TPU v7x, 256 devices: a whole 4x4x8 slice. The times are simulated.
256 devices in a mesh: wide: 64 (over z, x_hi, y), narrow: 4 (over x_lo, core).
Axes of the slice: x: 4 (x_hi: 2, x_lo: 2; x = x_hi * 2 + x_lo), y: 4, z: 8, core: 2. Of those that a mesh axis runs over, the one named last changes fastest.
Arguments:
- occupied: bfloat16 [512, 64, 4096], P('wide', 'narrow'), may hold values from -6 to 6
- empty: bfloat16 [1024, 64, 4096], P('wide', 'narrow'), may hold values from -6 to 6
- pair_occ: int32 [2048], P('wide'), may hold values from 0 to 7
- pair_emp: int32 [2048], P('wide'), may hold values from 0 to 15
- pair_level: int32 [2048], replicated, may hold values from 0 to 63
- denominators: float32 [64, 8], replicated, may hold values from 0.02 to 0.2
- trial: bfloat16 [131072, 512], P(('wide', 'narrow')), may hold values from -0.015625 to 0.015625
Outputs:
- response: bfloat16 [8, 131072, 512], P(None, ('wide', 'narrow'))
Inputs may be any that keep to these rules, and one draw needn't show every extreme that they name: Pair p uses occupied band (p // 32) * 8 + pair_occ[p]. Pair p uses empty band (p // 32) * 16 + pair_emp[p].
All inputs are finite; a program needn't handle non-finite values.
Results may differ from a plain program's by a relative error of at most 0.012.
Values may be sent and summed in bfloat16 or wider, within the bound.
A program may use at most 128 MiB of HBM per device.

v0:
```python
import math

import jax
import jax.numpy as jnp
from jax import lax
from jax.sharding import PartitionSpec as P

GRID = 64


def tables(grid_size):
    positions = jnp.arange(grid_size, dtype=jnp.int32)
    half_range = jnp.arange(grid_size // 2, dtype=jnp.int32)
    scaling = 1.0 / math.sqrt(grid_size)
    step_angle = 2.0 * math.pi / grid_size
    z_angles = (positions[:, None] * half_range[None, :] % grid_size).astype(
        jnp.float32
    ) * step_angle
    z_table = (
        jnp.stack([jnp.cos(z_angles), -jnp.sin(z_angles)], -1).reshape(grid_size, grid_size)
        * scaling
    )
    signed = jnp.where(half_range < grid_size // 4, half_range, half_range - grid_size // 2)
    y_angles = (signed[:, None] * positions[None, :] % grid_size).astype(jnp.float32) * step_angle
    y_table = jnp.stack([jnp.cos(y_angles), jnp.sin(y_angles)]) * scaling
    x_angles = (positions[:, None] * positions[None, :] % grid_size).astype(
        jnp.float32
    ) * step_angle
    x_table = jnp.stack([jnp.cos(x_angles), jnp.sin(x_angles)]) * scaling
    return (
        z_table.astype(jnp.bfloat16),
        y_table.astype(jnp.bfloat16),
        x_table.astype(jnp.bfloat16),
    )


def combine_parts(stacked):
    full_shape = stacked.shape[1:]
    halves = stacked.reshape(stacked.shape[:-1] + (stacked.shape[-1] // 2, 2))
    real_part = halves[0, ..., 0] + halves[1, ..., 1]
    imag_part = halves[0, ..., 1] - halves[1, ..., 0]
    return jnp.stack([real_part, imag_part], -1).reshape(full_shape)


def shards(occupied, empty, pair_occ, pair_emp, pair_level, denominators, trial):
    narrow_count = lax.axis_size("narrow")
    z_table, y_table, x_table = tables(GRID)
    planes = occupied.shape[1]
    pair_count = pair_occ.shape[0]
    occ_rows = jnp.take(occupied, pair_occ, axis=0)
    emp_rows = jnp.take(empty, pair_emp, axis=0)
    products = (occ_rows.astype(jnp.float32) * emp_rows.astype(jnp.float32)).astype(jnp.bfloat16)
    products = products.reshape(pair_count, planes, GRID, GRID)
    along_z = jnp.einsum(
        "pxyz,za->pxya", products, z_table, preferred_element_type=jnp.float32
    ).astype(jnp.bfloat16)
    along_y = combine_parts(
        jnp.einsum("sky,pxyq->spxkq", y_table, along_z, preferred_element_type=jnp.float32)
    ).astype(jnp.bfloat16)
    gathered = lax.all_to_all(along_y, "narrow", split_axis=3, concat_axis=1, tiled=True)
    summed = jnp.einsum("skx,pxyq->spkyq", x_table, gathered, preferred_element_type=jnp.float32)
    pair_waves = combine_parts(summed).astype(jnp.bfloat16).reshape(gathered.shape[0], -1)
    columns = lax.all_to_all(pair_waves, "wide", split_axis=1, concat_axis=0, tiled=True)
    block_width = columns.shape[1]
    wide_place = lax.axis_index("wide")
    narrow_place = lax.axis_index("narrow")
    block_depth = GRID // 2 // narrow_count
    flat_index = wide_place * block_width + jnp.arange(block_width, dtype=jnp.int32)
    channel = flat_index % (2 * block_depth)
    freq_y = flat_index // (2 * block_depth) % (GRID // 2)
    freq_x = flat_index // (2 * block_depth * (GRID // 2))
    freq_z = narrow_place * block_depth + channel // 2
    freq_x = jnp.where(freq_x < GRID // 2, freq_x, freq_x - GRID)
    freq_y = jnp.where(freq_y < GRID // 4, freq_y, freq_y - GRID // 2)
    squared = (freq_x * freq_x + freq_y * freq_y + freq_z * freq_z).astype(jnp.float32)
    quarter = float(GRID // 4)
    coulomb = 1.0 / jnp.sqrt(1.0 + squared / (quarter * quarter))
    scaled = (coulomb[:, None] * trial.astype(jnp.float32)).astype(jnp.bfloat16)
    partial_term = jnp.dot(columns, scaled, preferred_element_type=jnp.float32)
    projections = lax.psum(partial_term, ("wide", "narrow"))
    table_rows = jnp.arange(denominators.shape[0], dtype=jnp.int32)
    onehot = (pair_level[:, None] == table_rows[None, :]).astype(jnp.float32)
    weights = jnp.dot(onehot, denominators, precision=lax.Precision.HIGHEST)
    weighted = (jnp.transpose(weights)[:, :, None] * projections[None]).astype(jnp.bfloat16)
    response = jnp.einsum("pc,wpk->wck", columns, weighted, preferred_element_type=jnp.float32)
    return (response * coulomb[None, :, None]).astype(jnp.bfloat16)


def solution(mesh):
    placed = (
        P("wide", "narrow", None),
        P("wide", "narrow", None),
        P("wide"),
        P("wide"),
        P(),
        P(),
        P(("wide", "narrow"), None),
    )
    return jax.shard_map(
        shards,
        mesh=mesh,
        in_specs=placed,
        out_specs=P(None, ("wide", "narrow"), None),
        check_vma=False,
    )
```

profile of v0, /device:TPU:1, one launch (start us, length us, event | category | flops | bytes accessed | tf_op | source)
XLA Modules:
  0.0 582.4 jit_solution(12516573130424410726)
XLA Ops:
  6.5 0.0 copy-start
  6.5 0.8 compare_select_fusion.4
  7.3 0.7 compare_and_fusion
  8.0 0.7 compare_select_fusion.3
  8.7 0.1 sine_negate_fusion
  8.8 4.0 gather_fusion
  12.8 0.0 copy-done
  12.8 2.8 gather_fusion.1
  15.6 5.9 %multiply_convert_fusion.3 = bf16[32,16,4096]{2,1,0:T(8,128)(2,1)} fusion(bf16[32,16,4096]{2,1,0:T(8,128)(2,1)} %gather_fusion.1, bf16[32,16,4096]{2,1,0:T(8,128)(2,1)} %gather_fusion, pred[32]{0:T(512)(128)(4,1)S(1)} %get-tuple-element.13, pred[32]{0:T(512)(128)(4,1)S(1)} %get-tuple-element.14), kind=kLoop, calls=%fused_computation.17 | loop fusion | flops 12582912 | bytes 12582976 | tf_op jit(solution)/shard_map/convert_element_type | solution.py:52
  21.6 12.6 %convert_element_type.144 = bf16[32,16,64,64]{3,2,1,0:T(8,128)(2,1)} reshape(bf16[32,16,4096]{2,1,0:T(8,128)(2,1)} %multiply_convert_fusion.3) | data formatting | bytes 8388608 | tf_op jit(solution)/shard_map/convert_element_type | solution.py:52
  34.2 0.2 fusion.51
  34.3 10.4 %convolution_bitcast_fusion = f32[2,32,16,32,64]{4,3,0,2,1:T(8,128)} fusion(bf16[32,16,64,64]{3,2,1,0:T(8,128)(2,1)} %convert_element_type.144, bf16[64,64,1,1]{0,1,3,2:T(8,128)(2,1)S(1)} %bitcast.67, f32[1,32,64]{2,1,0:T(8,128)S(1)} %get-tuple-element.12, f32[1,32,64]{2,1,0:T(8,128)S(1)} %get-tuple-element.11), kind=kOutput, calls=%fused_computation.6 | convolution fusion | flops 538980352 | bytes 12607488 | tf_op jit(solution)/shard_map/sky,pxyq->spxkq/dot_general | solution.py:58
  44.7 24.2 %copy.44 = f32[2,32,16,32,64]{3,2,4,1,0:T(8,128)} copy(f32[2,32,16,32,64]{4,3,0,2,1:T(8,128)} %convolution_bitcast_fusion) | data formatting | bytes 16777216 | tf_op jit(solution)/shard_map/sky,pxyq->spxkq/transpose | solution.py:58
  68.9 14.1 %fusion.12 = (bf16[32,16,32,32,1]{2,1,3,0,4:T(8,128)(2,1)S(1)}, bf16[32,16,32,32,1]{2,1,3,0,4:T(8,128)(2,1)}) fusion(f32[2,32,16,32,32,2]{3,2,5,4,1,0:T(8,128)} %bitcast.59), kind=kLoop, calls=%fused_computation.20 | loop fusion | flops 2097152 | bytes 10485760 | tf_op jit(solution)/shard_map/add | solution.py:40
  83.0 7.3 %pad_maximum_fusion = bf16[32,16,32,32,2]{2,1,3,0,4:T(8,128)(2,1)} fusion(bf16[32,16,32,32,1]{2,1,3,0,4:T(8,128)(2,1)} %get-tuple-element.6, bf16[32,16,32,32,1]{2,1,3,0,4:T(8,128)(2,1)S(1)} %get-tuple-element.5), kind=kLoop, calls=%fused_computation.11 | loop fusion | flops 1048576 | bytes 4194304 | tf_op jit(solution)/shard_map/stack | solution.py:42
  90.3 8.3 %copy.47 = bf16[32,16,32,32,2]{2,1,4,3,0:T(8,128)(2,1)} copy(bf16[32,16,32,32,2]{2,1,3,0,4:T(8,128)(2,1)} %pad_maximum_fusion) | data formatting | bytes 4194304 | tf_op jit(solution)/shard_map/stack | solution.py:42
  98.7 9.1 %copy.92 = bf16[32,16,32,64]{2,1,0,3:T(8,128)(2,1)} copy(bf16[32,16,32,64]{2,1,3,0:T(8,128)(2,1)} %bitcast.63) | data formatting | bytes 4194304 | tf_op jit(solution)/shard_map/convert_element_type | solution.py:59
  107.7 10.8 %reshape.560 = bf16[4,2,131072]{2,1,0:T(2,128)(2,1)} reshape(bf16[64,32,16,32]{3,2,1,0:T(8,128)(2,1)} %bitcast.61) | data formatting | bytes 4194304
  118.6 6.8 %all-to-all-start = ((bf16[4,2,131072]{2,1,0:T(2,128)(2,1)}), bf16[4,2,131072]{2,1,0:T(2,128)(2,1)S(1)}, u32[]{:S(2)}, u32[]{:S(2)}) async-start(bf16[4,2,131072]{2,1,0:T(2,128)(2,1)} %reshape.560), calls=%async_computation | async-start | bytes 4194304 | tf_op jit(solution)/shard_map/all_to_all | solution.py:60
  125.3 0.1 fusion.41
  125.5 24.6 %all-to-all-done = bf16[4,2,131072]{2,1,0:T(2,128)(2,1)S(1)} async-done(((bf16[4,2,131072]{2,1,0:T(2,128)(2,1)}), bf16[4,2,131072]{2,1,0:T(2,128)(2,1)S(1)}, u32[]{:S(2)}, u32[]{:S(2)}) %all-to-all-start) | async-done | bytes 2097184 | tf_op jit(solution)/shard_map/all_to_all | solution.py:60
  150.0 5.6 reshape.561
  155.6 16.3 %copy.50 = bf16[32,4,16,32,16]{3,4,2,1,0:T(8,128)(2,1)} copy(bf16[32,4,16,32,16]{3,2,0,4,1:T(8,128)(2,1)} %bitcast.62) | data formatting | bytes 4194304 | tf_op jit(solution)/shard_map/all_to_all | solution.py:60
  172.0 17.1 %fusion.6 = f32[32,32,16,2,64]{4,1,3,2,0:T(8,128)S(1)} fusion(bf16[32,64,32,16,1]{2,3,1,0,4:T(8,128)(2,1)} %bitcast.60, f32[1,64,64]{2,1,0:T(8,128)S(1)} %get-tuple-element.17, f32[1,64,64]{2,1,0:T(8,128)S(1)} %get-tuple-element.18), kind=kOutput, calls=%fused_computation.13 | convolution fusion | flops 268460032 | bytes 10518528 | tf_op jit(solution)/shard_map/skx,pxyq->spkyq/dot_general | solution.py:61
  189.1 6.2 %fusion.73 = (f32[1,32,64,32,8,1]{2,3,0,5,4,1:T(8,128)}, f32[1,32,64,32,8,1]{2,3,0,5,4,1:T(8,128)}, f32[1,32,64,32,8,1]{2,3,0,5,4,1:T(8,128)}, f32[1,32,64,32,8,1]{2,3,0,5,4,1:T(8,128)}) fusion(f32[2,32,64,32,8,2]{2,3,0,5,4,1:T(8,128)S(1)} %bitcast.58), kind=kLoop, calls=%fused_computation.125 | loop fusion | bytes 16777216 | tf_op jit(solution)/shard_map/slice | solution.py:40
  195.3 0.0 copy-start.2
  195.3 0.0 copy-start.3
  195.3 8.2 %fusion.16 = bf16[32,64,32,8,1]{1,0,4,3,2:T(8,128)(2,1)S(1)} fusion(f32[1,32,64,32,8,1]{2,3,0,5,4,1:T(8,128)} %get-tuple-element.9, f32[1,32,64,32,8,1]{2,3,0,5,4,1:T(8,128)} %get-tuple-element.7), kind=kLoop, calls=%fused_computation.28 | loop fusion | flops 1048576 | bytes 5242880 | tf_op jit(solution)/shard_map/add | solution.py:40
  203.5 0.0 copy-done.2
  203.5 0.0 copy-done.3
  203.5 4.6 fusion.17
  208.1 2.8 pad_maximum_fusion.1
  210.9 0.0 copy-start.5
  210.9 6.9 %copy.56 = bf16[32,64,512]{2,0,1:T(8,128)(2,1)} copy(bf16[32,64,512]{1,0,2:T(8,128)(2,1)} %bitcast.64) | data formatting | bytes 4194304 | tf_op jit(solution)/shard_map/convert_element_type | solution.py:62
  217.8 12.6 %all-to-all-start.1 = ((bf16[32,64,512]{2,0,1:T(8,128)(2,1)}), bf16[32,64,512]{2,0,1:T(8,128)(2,1)S(1)}, u32[]{:S(2)}, u32[]{:S(2)}) async-start(bf16[32,64,512]{2,0,1:T(8,128)(2,1)} %copy.56), calls=%async_computation.1 | async-start | bytes 4194304 | tf_op jit(solution)/shard_map/all_to_all | solution.py:63
  230.4 0.0 all-reduce.2.cloned.1.call-start
  230.5 48.0 %all-to-all-done.1 = bf16[32,64,512]{2,0,1:T(8,128)(2,1)S(1)} async-done(((bf16[32,64,512]{2,0,1:T(8,128)(2,1)}), bf16[32,64,512]{2,0,1:T(8,128)(2,1)S(1)}, u32[]{:S(2)}, u32[]{:S(2)}) %all-to-all-start.1) | async-done | bytes 2097184 | tf_op jit(solution)/shard_map/all_to_all | solution.py:63
  278.5 0.0 copy-start.4
  278.5 0.0 copy-done.5
  278.5 3.3 fusion.18
  281.8 0.0 copy-done.4
  281.8 0.0 copy-start.6
  281.8 0.0 copy-start.7
  281.8 0.0 all-reduce.2.cloned.1.call-update
  281.9 0.7 copy-done.6
  282.5 0.0 copy-done.7
  282.5 0.9 convolution_bitcast_fusion.1
  283.5 266.4 %all-reduce.2.cloned.1.call-done = f32[2048,512]{1,0:T(8,128)} async-done(((f32[2048,512]{1,0:T(8,128)}), f32[2048,512]{1,0:T(8,128)}) %all-reduce.2.cloned.1.call-update) | async-done | bytes 4194320 | tf_op jit(solution)/shard_map/psum | solution.py:80
  549.9 5.3 copy.57
  555.2 0.0 copy-start.1
  555.2 13.7 %fusion.11 = bf16[8,512,512]{1,2,0:T(8,128)(2,1)} fusion(f32[512]{0:T(512)S(1)} %fusion.68, bf16[2048,512,1]{1,0,2:T(8,128)(2,1)} %bitcast.66, f32[2048,512]{0,1:T(8,128)} %copy.57, f32[8,2048]{1,0:T(8,128)S(1)} %convolution_bitcast_fusion.1), kind=kOutput, calls=%fused_computation.19 | convolution fusion | flops 8610906112 | bytes 10553344 | tf_op jit(solution)/shard_map/pc,wpk->wck/dot_general | solution.py:85
  568.9 6.4 %copy.58 = bf16[8,512,512]{2,1,0:T(8,128)(2,1)} copy(bf16[8,512,512]{1,2,0:T(8,128)(2,1)} %fusion.11) | data formatting | bytes 8388608 | tf_op jit(solution)/shard_map/convert_element_type | solution.py:86
  575.3 0.0 copy-done.1
  (6 shorter events, 0.1 us)
Async XLA Ops:
  6.5 6.3 %copy-start = (bf16[16,16,4096]{2,1,0:T(8,128)(2,1)S(1)}, bf16[16,16,4096]{2,1,0:T(8,128)(2,1)}, u32[]{:S(2)}) copy-start(bf16[16,16,4096]{2,1,0:T(8,128)(2,1)} %param.8) | copy-start | bytes 6291460
  118.6 31.5 %all-to-all-start = ((bf16[4,2,131072]{2,1,0:T(2,128)(2,1)}), bf16[4,2,131072]{2,1,0:T(2,128)(2,1)S(1)}, u32[]{:S(2)}, u32[]{:S(2)}) async-start(bf16[4,2,131072]{2,1,0:T(2,128)(2,1)} %reshape.560), calls=%async_computation | async-start | bytes 4194304 | tf_op jit(solution)/shard_map/all_to_all | solution.py:60
  195.3 8.2 %copy-start.2 = (f32[1,32,64,32,8,1]{2,3,0,5,4,1:T(8,128)S(1)}, f32[1,32,64,32,8,1]{2,3,0,5,4,1:T(8,128)}, u32[]{:S(2)}) copy-start(f32[1,32,64,32,8,1]{2,3,0,5,4,1:T(8,128)} %get-tuple-element.8) | copy-start | bytes 6291460
  195.3 8.2 %copy-start.3 = (f32[1,32,64,32,8,1]{2,3,0,5,4,1:T(8,128)S(1)}, f32[1,32,64,32,8,1]{2,3,0,5,4,1:T(8,128)}, u32[]{:S(2)}) copy-start(f32[1,32,64,32,8,1]{2,3,0,5,4,1:T(8,128)} %get-tuple-element.10) | copy-start | bytes 6291460
  210.9 67.6 %copy-start.5 = (bf16[512,512]{1,0:T(8,128)(2,1)S(1)}, bf16[512,512]{1,0:T(8,128)(2,1)}, u32[]{:S(2)}) copy-start(bf16[512,512]{1,0:T(8,128)(2,1)} %param.13) | copy-start | bytes 1572868
  217.8 60.7 %all-to-all-start.1 = ((bf16[32,64,512]{2,0,1:T(8,128)(2,1)}), bf16[32,64,512]{2,0,1:T(8,128)(2,1)S(1)}, u32[]{:S(2)}, u32[]{:S(2)}) async-start(bf16[32,64,512]{2,0,1:T(8,128)(2,1)} %copy.56), calls=%async_computation.1 | async-start | bytes 4194304 | tf_op jit(solution)/shard_map/all_to_all | solution.py:63
  230.4 319.5 %all-reduce.2.cloned.1.call-start = ((), (), s32[]{:S(2)}) async-start(), calls=%async_computation.2 | async-start | bytes 8388608 | tf_op jit(solution)/shard_map/psum | solution.py:80
  278.5 3.4 copy-start.4
  281.8 0.7 copy-start.6
  281.8 0.7 copy-start.7
  555.2 20.1 %copy-start.1 = (bf16[16,16,4096]{2,1,0:T(8,128)(2,1)S(1)}, bf16[16,16,4096]{2,1,0:T(8,128)(2,1)}, u32[]{:S(2)}) copy-start(bf16[16,16,4096]{2,1,0:T(8,128)(2,1)} %param.8) | copy-start | bytes 6291460
Sparse Core Ops, SparseCore 0:
  282.0 267.8 all-reduce.1
where the time goes:
time: 589 us; the launch traced here: 582 us
  waiting for transfers between devices  339 us (58%)
  local copies, waits for them, and re-layouts  119 us (20%)
  other arithmetic  45.5 us (8%)
  matrix products  45.3 us (8%)
  starting transfers between devices  19.4 us (3%)
  between operations  13.7 us (2%)
    psum x1, waiting for transfers between devices, shards(): projections = lax.psum(partial_term, ('wide', 'narrow'))  266 us
    all_to_all x1, waiting for transfers between devices, shards(): lax.all_to_all(pair_waves, 'wide', split_axis=1, concat_axis=0, tiled=True)  48 us
    all_to_all x1, waiting for transfers between devices, shards(): lax.all_to_all(along_y, 'narrow', split_axis=3, concat_axis=1, tiled=True)  24.6 us
    transpose x1, local copies, waits for them, and re-layouts, shards(): jnp.einsum('sky,pxyq->spxkq', y_table, along_z, preferred_element_type=jn...  24.2 us
    add x2, other arithmetic, combine_parts(): real_part = halves[0, ..., 0] + halves[1, ..., 1]  22.3 us
    unnamed x18, local copies, waits for them, and re-layouts  17.1 us
    dot_general x1, matrix products, shards(): jnp.einsum('skx,pxyq->spkyq', x_table, gathered, preferred_element_type=j...  17.1 us
    all_to_all x1, local copies, waits for them, and re-layouts, shards(): lax.all_to_all(along_y, 'narrow', split_axis=3, concat_axis=1, tiled=True)  16.3 us
  transfers between devices with their start and end apart: 3, of which 3 were waited for; matrix products, arithmetic and copies ran while one was open for 0% of the time, Pallas kernels for 0%

commit v1 on v0

v1 whole, which is shorter than its diff:
```python
import math

import jax
import jax.numpy as jnp
import ml_dtypes
import numpy as np
from jax import lax
from jax.experimental import pallas as pl
from jax.experimental.pallas import tpu as pltpu
from jax.sharding import PartitionSpec as P

GRID = 64
MESH = pl.DeviceIdType.MESH
F32, BF16 = jnp.float32, jnp.bfloat16
LIMIT = 60 * 1024 * 1024


def rounded(values):
    return values.astype(np.float32).astype(ml_dtypes.bfloat16).astype(np.float32)


def tables():
    at = np.arange(GRID)
    half = np.arange(GRID // 2)
    scaling = 1.0 / math.sqrt(GRID)
    step = 2.0 * math.pi / GRID
    z_angles = (at[:, None] * half[None, :] % GRID) * step
    z_real = rounded(scaling * np.cos(z_angles))
    z_imag = rounded(-scaling * np.sin(z_angles))
    signed = np.where(half < GRID // 4, half, half - GRID // 2)
    y_angles = (signed[:, None] * at[None, :] % GRID) * step
    y_cos = rounded(scaling * np.cos(y_angles))
    y_sin = rounded(scaling * np.sin(y_angles))
    x_angles = (at[:, None] * at[None, :] % GRID) * step
    x_cos = rounded(scaling * np.cos(x_angles))
    x_sin = rounded(scaling * np.sin(x_angles))
    zr = z_real.reshape(GRID, 4, 8).transpose(1, 0, 2)
    zi = z_imag.reshape(GRID, 4, 8).transpose(1, 0, 2)

    def spread(first, second):
        both = np.stack([first, second], 2)[:, :, :, None, :]
        return np.broadcast_to(both, (4, GRID, 2, 16, 8)).reshape(4, GRID, 256)

    z_first = spread(zr, zi)
    z_second = spread(zi, -zr)

    def widen(table):
        table = table[:, :32].reshape(16, 2, 32).transpose(1, 2, 0)
        return np.broadcast_to(table[:, :, None, :, None], (2, 32, 2, 16, 8)).reshape(2, 32, 256)

    x_table = np.block([[x_cos, x_sin], [-x_sin, x_cos]])
    perm = np.zeros((512, 512), np.float32)
    part, parity, j16, kz8 = np.meshgrid(np.arange(2), np.arange(2), np.arange(16), np.arange(8), indexing="ij")
    inner = np.arange(512)
    outer = ((2 * j16 + parity) * 16 + 2 * kz8 + part).reshape(-1)
    perm[outer, inner] = 1.0
    small = [z_first, z_second, widen(y_cos), widen(y_sin), x_table, perm]
    return [np.ascontiguousarray(t).astype(ml_dtypes.bfloat16) for t in small]


def plane_kernel(occ_at, emp_at, occ_ref, emp_ref, z_first, z_second, y_cos, y_sin, out_ref, x_scr, w_scr):
    @pl.loop(0, 32)
    def _(pair):
        product = occ_ref[occ_at[pair]].astype(F32) * emp_ref[emp_at[pair]].astype(F32)
        low, high = product[:, :2048], product[:, 2048:]
        rows = pl.ds(pl.multiple_of(pair * 16, 16), 16)
        x_scr[0, rows, :] = (low + high).astype(BF16)
        x_scr[1, rows, :] = (low - high).astype(BF16)

    for parity in range(2):
        for n in range(4):
            first = z_first[n].astype(F32)
            second = z_second[n].astype(F32)

            @pl.loop(0, 4)
            def _(group):
                cos8 = y_cos[parity, pl.ds(pl.multiple_of(group * 8, 8), 8), :].astype(F32)
                sin8 = y_sin[parity, pl.ds(pl.multiple_of(group * 8, 8), 8), :].astype(F32)
                for inner in range(8):
                    rows = pl.ds(pl.multiple_of(group * 512 + inner * 64, 64), 64)
                    w_scr[parity * 4 + n, rows, :] = (
                        first * cos8[inner : inner + 1] + second * sin8[inner : inner + 1]
                    ).astype(BF16)

    for parity in range(2):

        @pl.loop(0, 4)
        def _(n):
            out_ref[n, :, parity * 256 : (parity + 1) * 256] = jnp.dot(
                x_scr[parity], w_scr[parity * 4 + n], preferred_element_type=F32
            ).astype(BF16)


def planes(pair_occ, pair_emp, occupied, empty, z_first, z_second, y_cos, y_sin):
    smem = pl.BlockSpec(memory_space=pltpu.SMEM)
    vmem = pl.BlockSpec(memory_space=pltpu.VMEM)
    return pl.pallas_call(
        plane_kernel,
        out_shape=jax.ShapeDtypeStruct((4, 512, 512), BF16),
        in_specs=[smem, smem] + [vmem] * 6,
        out_specs=vmem,
        scratch_shapes=[pltpu.VMEM((2, 512, 2048), BF16), pltpu.VMEM((8, 2048, 256), BF16)],
        compiler_params=pltpu.CompilerParams(vmem_limit_bytes=LIMIT),
        name="planes",
    )(pair_occ, pair_emp, occupied, empty, z_first, z_second, y_cos, y_sin)


def x_kernel(in_ref, table_ref, out_ref, scr):
    @pl.loop(0, 32)
    def _(pair):
        rows = pl.ds(pl.multiple_of(pair * 16, 16), 16)
        stacked = jnp.concatenate(
            [
                jnp.concatenate(
                    [in_ref[n, rows, e * 256 + part * 128 : e * 256 + part * 128 + 128] for e in range(2)], 1
                )
                for part in range(2)
                for n in range(4)
            ],
            0,
        )
        waves = jnp.dot(table_ref[...], stacked, preferred_element_type=F32)
        for part in range(2):
            scr_part = scr.at[part]
            scr_part[pl.ds(pair, 64, stride=32), :] = waves[part * 64 : part * 64 + 64, 0:128]
            scr_part = scr.at[2 + part]
            scr_part[pl.ds(pair, 64, stride=32), :] = waves[part * 64 : part * 64 + 64, 128:256]

    @pl.loop(0, 16)
    def _(group):
        rows = pl.ds(pl.multiple_of(group * 128, 128), 128)
        for part in range(2):
            for e in range(2):
                out_ref[rows, (part * 2 + e) * 128 : (part * 2 + e) * 128 + 128] = scr[e * 2 + part, rows, :].astype(
                    BF16
                )


def along_x(gathered, x_table):
    vmem = pl.BlockSpec(memory_space=pltpu.VMEM)
    return pl.pallas_call(
        x_kernel,
        out_shape=jax.ShapeDtypeStruct((2048, 512), BF16),
        in_specs=[vmem] * 2,
        out_specs=vmem,
        scratch_shapes=[pltpu.VMEM((4, 2048, 128), F32)],
        compiler_params=pltpu.CompilerParams(vmem_limit_bytes=LIMIT),
        name="along_x",
    )(gathered, x_table)


def place():
    wide, narrow = lax.axis_index("wide"), lax.axis_index("narrow")
    z, x_hi, y = wide // 8, wide // 4 % 2, wide % 4
    x_lo, core = narrow // 2, narrow % 2
    return x_hi * 2 + x_lo, y, z, core


def device(x, y, z, core):
    return (z * 8 + x // 2 * 4 + y, x % 2 * 2 + core)


def sum_kernel(
    part_ref, out_ref, core_send, core_recv, acc, far_send, far_recv, near_send, near_recv,
    low_send, low_recv, z_send, z_recv, send_sem, recv_sem,
):
    x, y, z, core = place()
    mate = device(x, y, z, 1 - core)
    shifts = (
        [device((x + 1) % 4, y, z, core), device((x + 3) % 4, y, z, core)],
        [device(x, (y + 1) % 4, z, core), device(x, (y + 3) % 4, z, core)],
    )
    z_mates = [device(x, y, (z + step) % 8, core) for step in range(1, 8)]
    barrier = pltpu.get_barrier_semaphore()
    peers = [mate] + shifts[0] + shifts[1] + z_mates
    for peer in peers:
        pl.semaphore_signal(barrier, inc=1, device_id=peer, device_id_type=MESH)
    pl.semaphore_wait(barrier, len(peers))

    count = [0]
    sent = []

    def send(src, dst, peer):
        at = count[0]
        count[0] += 1
        copy = pltpu.make_async_remote_copy(
            src_ref=src, dst_ref=dst, send_sem=send_sem.at[at], recv_sem=recv_sem.at[at],
            device_id=peer, device_id_type=MESH,
        )
        copy.start()
        sent.append(copy)
        return copy

    def tile(start, size):
        return pl.ds(pl.multiple_of(start, 16), size)

    other = pl.ds(pl.multiple_of((1 - core) * 256, 256), 256)
    core_copies = []
    for piece in range(4):
        rows = pl.ds(piece * 512, 512)
        core_send[rows, :] = part_ref[rows, other].astype(BF16)
        core_copies.append(send(core_send.at[rows], core_recv.at[rows], mate))
    for piece in range(4):
        rows = pl.ds(piece * 512, 512)
        core_copies[piece].wait_recv()
        for h in range(2):
            mine = pl.ds(pl.multiple_of(core * 256 + h * 128, 128), 128)
            acc[h, rows, :] = part_ref[rows, mine] + core_recv[rows, h * 128 : h * 128 + 128].astype(F32)

    first = (x, y)
    second = (y, x)
    base = [0, 0]
    for stage in range(2):
        size = 512 if stage == 0 else 128
        half = size // 2
        me = first if stage == 0 else second
        far = {}
        start = {}
        for h in range(2):
            axis = h if stage == 0 else 1 - h
            up, down = shifts[axis]

            def block(at, h=h, me=me, size=size):
                return base[h] + (me[h] + at) % 4 * size

            start[h] = block
            far_send[stage, h, 0:half] = acc[h, tile(block(2), half), :].astype(BF16)
            far_send[stage, h, 256 : 256 + half] = acc[h, tile(block(2) + half, half), :].astype(BF16)
            far[h] = (
                send(far_send.at[stage, h, pl.ds(0, half)], far_recv.at[stage, h, pl.ds(0, half)], up),
                send(far_send.at[stage, h, pl.ds(256, half)], far_recv.at[stage, h, pl.ds(256, half)], down),
            )
        near = {}
        for h in range(2):
            axis = h if stage == 0 else 1 - h
            up, down = shifts[axis]
            block = start[h]
            near_send[stage, h, 0, half:size] = acc[h, tile(block(1) + half, half), :].astype(BF16)
            near_send[stage, h, 1, 0:half] = acc[h, tile(block(3), half), :].astype(BF16)
            far[h][0].wait_recv()
            near_send[stage, h, 0, 0:half] = (
                acc[h, tile(block(1), half), :] + far_recv[stage, h, 0:half].astype(F32)
            ).astype(BF16)
            to_up = send(near_send.at[stage, h, 0, pl.ds(0, size)], near_recv.at[stage, h, 0, pl.ds(0, size)], up)
            far[h][1].wait_recv()
            near_send[stage, h, 1, half:size] = (
                acc[h, tile(block(3) + half, half), :] + far_recv[stage, h, 256 : 256 + half].astype(F32)
            ).astype(BF16)
            to_down = send(near_send.at[stage, h, 1, pl.ds(0, size)], near_recv.at[stage, h, 1, pl.ds(0, size)], down)
            near[h] = (to_up, to_down)
        for h in range(2):
            block = start[h]
            near[h][0].wait_recv()
            near[h][1].wait_recv()
            rows = tile(block(0), size)
            acc[h, rows, :] = (
                acc[h, rows, :]
                + near_recv[stage, h, 0, 0:size].astype(F32)
                + near_recv[stage, h, 1, 0:size].astype(F32)
            )
            base[h] = block(0)

    copies = []
    for step in range(1, 8):
        for h in range(2):
            z_send[step, h] = acc[h, tile(base[h] + (z + step) % 8 * 16, 16), :].astype(BF16)
        copies.append(send(z_send.at[step], z_recv.at[step], z_mates[step - 1]))
    total = [acc[h, tile(base[h] + z * 16, 16), :] for h in range(2)]
    for step in range(1, 8):
        copies[step - 1].wait_recv()
        for h in range(2):
            total[h] = total[h] + z_recv[step, h].astype(F32)

    for h in range(2):
        low_send[h] = total[h].astype(BF16)
        out_ref[core * 2 + h, tile(base[h] + z * 16, 16), :] = low_send[h]
    copies = []
    for step in range(1, 8):
        copies.append(send(low_send, low_recv.at[step], z_mates[step - 1]))
    for step in range(1, 8):
        copies[step - 1].wait_recv()
        for h in range(2):
            out_ref[core * 2 + h, tile(base[h] + (z + 8 - step) % 8 * 16, 16), :] = low_recv[step, h]
    for stage in (1, 0):
        size = 512 if stage == 0 else 128
        half = size // 2
        me = first if stage == 0 else second
        outer = [base[h] - me[h] * size for h in range(2)]
        near = {}
        for h in range(2):
            axis = h if stage == 0 else 1 - h
            up, down = shifts[axis]
            mine = out_ref.at[core * 2 + h, tile(base[h], size)]
            near[h] = (send(mine, mine, up), send(mine, mine, down))
        far = {}
        for h in range(2):
            axis = h if stage == 0 else 1 - h
            up, down = shifts[axis]
            near[h][0].wait_recv()
            piece = out_ref.at[core * 2 + h, tile(outer[h] + (me[h] + 3) % 4 * size, half)]
            to_up = send(piece, piece, up)
            near[h][1].wait_recv()
            piece = out_ref.at[core * 2 + h, tile(outer[h] + (me[h] + 1) % 4 * size + half, half)]
            far[h] = (to_up, send(piece, piece, down))
        for h in range(2):
            far[h][0].wait_recv()
            far[h][1].wait_recv()
            base[h] = outer[h]
    for h in range(2):
        mine = out_ref.at[core * 2 + h]
        send(mine, mine, mate).wait_recv()
    for copy in sent:
        copy.wait_send()


def sum_projections(partial_term):
    vmem = pl.BlockSpec(memory_space=pltpu.VMEM)
    copies = 4 + 8 * 2 + 7 + 7 + 8 + 8 + 2
    return pl.pallas_call(
        sum_kernel,
        out_shape=jax.ShapeDtypeStruct((4, 2048, 128), BF16),
        in_specs=[vmem],
        out_specs=vmem,
        scratch_shapes=[
            pltpu.VMEM((2048, 256), BF16),
            pltpu.VMEM((2048, 256), BF16),
            pltpu.VMEM((2, 2048, 128), F32),
            pltpu.VMEM((2, 2, 512, 128), BF16),
            pltpu.VMEM((2, 2, 512, 128), BF16),
            pltpu.VMEM((2, 2, 2, 512, 128), BF16),
            pltpu.VMEM((2, 2, 2, 512, 128), BF16),
            pltpu.VMEM((2, 16, 128), BF16),
            pltpu.VMEM((8, 2, 16, 128), BF16),
            pltpu.VMEM((8, 2, 16, 128), BF16),
            pltpu.VMEM((8, 2, 16, 128), BF16),
            pltpu.SemaphoreType.DMA((copies,)),
            pltpu.SemaphoreType.DMA((copies,)),
        ],
        compiler_params=pltpu.CompilerParams(vmem_limit_bytes=LIMIT, collective_id=0, has_side_effects=True),
        name="sum_projections",
    )(partial_term)


def response_kernel(waves_ref, perm_ref, weights_ref, proj_ref, coulomb_ref, out_ref, turned):
    w = pl.program_id(0)

    @pl.when(w == 0)
    def _():
        for piece in range(4):
            turned[:, piece * 512 : piece * 512 + 512] = lax.dot_general(
                perm_ref[...],
                waves_ref[piece * 512 : piece * 512 + 512, :],
                (((1,), (1,)), ((), ())),
                preferred_element_type=F32,
            ).astype(BF16)

    lanes = lax.broadcasted_iota(jnp.int32, (256, 8), 1)
    total = jnp.zeros((512, 512), F32)
    for piece in range(8):
        rows = slice(piece * 256, piece * 256 + 256)
        column = jnp.sum(jnp.where(lanes == w, weights_ref[rows, :], 0.0), axis=1, keepdims=True)
        weighted = jnp.concatenate(
            [(proj_ref[block, rows, :].astype(F32) * column).astype(BF16) for block in range(4)], 1
        )
        total += jnp.dot(turned[:, rows], weighted, preferred_element_type=F32)
    out_ref[0] = (total * coulomb_ref[...]).astype(BF16)


def respond(waves, perm, weights, projections, coulomb):
    def whole(*shape):
        return pl.BlockSpec(shape, lambda w: (0,) * len(shape))

    return pl.pallas_call(
        response_kernel,
        out_shape=jax.ShapeDtypeStruct((8, 512, 512), BF16),
        grid=(8,),
        in_specs=[whole(2048, 512), whole(512, 512), whole(2048, 8), whole(4, 2048, 128), whole(512, 1)],
        out_specs=pl.BlockSpec((1, 512, 512), lambda w: (w, 0, 0)),
        scratch_shapes=[pltpu.VMEM((512, 2048), BF16)],
        compiler_params=pltpu.CompilerParams(vmem_limit_bytes=LIMIT),
        name="respond",
    )(waves, perm, weights, projections, coulomb)


def shards(occupied, empty, pair_occ, pair_emp, pair_level, denominators, trial):
    z_first, z_second, y_cos, y_sin, x_table, perm = [jnp.asarray(t) for t in tables()]
    blocks = planes(pair_occ, pair_emp, occupied, empty, z_first, z_second, y_cos, y_sin)
    gathered = lax.all_to_all(blocks, "narrow", split_axis=0, concat_axis=0, tiled=True)
    waves = along_x(gathered, x_table).reshape(64, 32, 512)
    columns = lax.all_to_all(waves, "wide", split_axis=0, concat_axis=0, tiled=True).reshape(2048, 512)

    freq_x = lax.axis_index("wide")
    freq_x = jnp.where(freq_x < GRID // 2, freq_x, freq_x - GRID)
    at = jnp.arange(512, dtype=jnp.int32)
    freq_y = at // 16
    freq_y = jnp.where(freq_y < GRID // 4, freq_y, freq_y - GRID // 2)
    freq_z = lax.axis_index("narrow") * 8 + at % 16 // 2
    squared = (freq_x * freq_x + freq_y * freq_y + freq_z * freq_z).astype(F32)
    quarter = float(GRID // 4)
    coulomb = (1.0 / jnp.sqrt(1.0 + squared / (quarter * quarter)))[:, None]
    scaled = (coulomb * trial.astype(F32)).astype(BF16)
    scaled = jnp.dot(perm.T, scaled, preferred_element_type=F32).astype(BF16)
    partial_term = jnp.dot(columns, scaled, preferred_element_type=F32)
    projections = sum_projections(partial_term)
    rows = jnp.arange(denominators.shape[0], dtype=jnp.int32)
    onehot = (pair_level[:, None] == rows[None, :]).astype(F32)
    weights = jnp.dot(onehot, denominators, precision=lax.Precision.HIGHEST)
    return respond(columns, perm, weights, projections, coulomb)


def solution(mesh):
    placed = (
        P("wide", "narrow", None),
        P("wide", "narrow", None),
        P("wide"),
        P("wide"),
        P(),
        P(),
        P(("wide", "narrow"), None),
    )
    return jax.shard_map(
        shards,
        mesh=mesh,
        in_specs=placed,
        out_specs=P(None, ("wide", "narrow"), None),
        check_vma=False,
    )
```

time: 589 us -> 195 us (0.33); the launches traced: 582 us -> 195 us
  waiting for transfers between devices: 339 us -> 45.3 us
  local copies, waits for them, and re-layouts: 119 us -> 0.02 us
  Pallas kernels: 0 us -> 98.2 us
  other arithmetic: 45.5 us -> 0.89 us
  matrix products: 45.3 us -> 5.53 us
  blocking collectives: 0 us -> 32.3 us
  between operations: 13.7 us -> 0.04 us
  starting transfers between devices: 19.4 us -> 12.7 us
    psum x1 -> x0, waiting for transfers between devices: 266 us -> none  [shards(): projections = lax.psum(partial_term, ('wide', 'narrow'))]
    pallas_call x0 -> x4, Pallas kernels: none -> 98.2 us  [the longest x1 57.3 us: sum_projections(): pl.pallas_call(sum_kernel, out_shape=jax.ShapeDtypeStruct((4, 2048, 128),...]
    dot_general x4 -> x1, matrix products: 44.4 us -> 3.83 us  [shards(): partial_term = jnp.dot(columns, scaled, preferred_element_type=F32)]
    convert_element_type x5 -> x0, local copies, waits for them, and re-layouts: 35 us -> none  [the longest x1 12.6 us: shards(): (occ_rows.astype(jnp.float32) * emp_rows.astype(jnp.float32)).astype(jnp....]
    all_to_all x0 -> x1, blocking collectives: none -> 32.3 us  [shards(): lax.all_to_all(blocks, 'narrow', split_axis=0, concat_axis=0, tiled=True)]
    all_to_all x2 -> x1, waiting for transfers between devices: 72.6 us -> 45.3 us  [shards(): lax.all_to_all(waves, 'wide', split_axis=0, concat_axis=0, tiled=True)]
    transpose x1 -> x0, local copies, waits for them, and re-layouts: 24.2 us -> none  [shards(): jnp.einsum('sky,pxyq->spxkq', y_table, along_z, preferred_element_type=jn...]
    add x2 -> x0, other arithmetic: 22.3 us -> none  [combine_parts(): real_part = halves[0, ..., 0] + halves[1, ..., 1]]
  transfers between devices with their start and end apart: 3 -> 1, of which waited for: 3 -> 1; matrix products, arithmetic and copies ran while one was open for 0% -> 1% of each run, Pallas kernels for 0% -> 0%
where the time goes in v1:
time: 195 us
  Pallas kernels  98.2 us (50%)
  waiting for transfers between devices  45.3 us (23%)
  blocking collectives  32.3 us (17%)
  starting transfers between devices  12.7 us (7%)
  matrix products  5.53 us (3%)
    pallas_call x1, Pallas kernels, sum_projections(): pl.pallas_call(sum_kernel, out_shape=jax.ShapeDtypeStruct((4, 2048, 128),...  57.3 us
    all_to_all x1, waiting for transfers between devices, shards(): lax.all_to_all(waves, 'wide', split_axis=0, concat_axis=0, tiled=True)  45.3 us
    all_to_all x1, blocking collectives, shards(): lax.all_to_all(blocks, 'narrow', split_axis=0, concat_axis=0, tiled=True)  32.3 us
    pallas_call x1, Pallas kernels, respond(): pl.pallas_call(response_kernel, out_shape=jax.ShapeDtypeStruct((8, 512, 5...  15.8 us
    pallas_call x1, Pallas kernels, planes(): pl.pallas_call(plane_kernel, out_shape=jax.ShapeDtypeStruct((4, 512, 512)...  13.3 us
    all_to_all x1, starting transfers between devices, shards(): lax.all_to_all(waves, 'wide', split_axis=0, concat_axis=0, tiled=True)  12.7 us
    pallas_call x1, Pallas kernels, along_x(): pl.pallas_call(x_kernel, out_shape=jax.ShapeDtypeStruct((2048, 512), BF16...  11.7 us
  transfers between devices with their start and end apart: 1, of which 1 were waited for; matrix products, arithmetic and copies ran while one was open for 1% of the time, Pallas kernels for 0%

profile of v1, /device:TPU:1, one launch (start us, length us, event | category | flops | bytes accessed | tf_op | source)
XLA Modules:
  0.0 195.0 jit_solution(10172524624004859584)
XLA Ops:
  0.0 0.0 copy-start
  0.0 13.3 %planes.1 = bf16[4,512,512]{2,1,0:T(8,128)(2,1)} custom-call(s32[32]{0:T(128)} %occ_at.1, s32[32]{0:T(128)} %emp_at.1, bf16[8,16,4096]{2,1,0:T(8,128)(2,1)} %occ_ref.1, bf16[16,16,4096]{2,1,0:T(8,128)(2,1)} %emp_ref.1, bf16[4,64,256]{2,1,0:T(8,128)(2,1)} %constant.77.clone.z_first, bf16[4,64,256]{2,1,0:T(8,128)(2,1)} %constant.78.clone.z_second, ...), custom_call_target="tpu_custom_call" | custom-call | tf_op jit(solution)/shard_map/planes/pallas_call | solution.py:97
  13.3 32.3 %all_to_all.10.in_ref = bf16[4,512,512]{2,1,0:T(8,128)(2,1)} all-to-all(bf16[4,512,512]{2,1,0:T(8,128)(2,1)} %planes.1), channel_id=1, replica_groups=mesh['wide'=64,'narrow'=4] {'narrow'}, dimensions={0} | all-to-all | bytes 4194304 | tf_op jit(solution)/shard_map/all_to_all | solution.py:388
  45.6 11.7 %along_x.1 = bf16[2048,512]{1,0:T(8,128)(2,1)} custom-call(bf16[4,512,512]{2,1,0:T(8,128)(2,1)} %all_to_all.10.in_ref, bf16[128,128]{1,0:T(8,128)(2,1)} %constant.81.clone.table_ref), custom_call_target="tpu_custom_call" | custom-call | tf_op jit(solution)/shard_map/along_x/pallas_call | solution.py:141
  57.3 0.0 copy-start.3
  57.3 0.0 copy-start.2
  57.3 0.0 copy-start.4
  57.3 12.7 %all-to-all-start.1 = ((bf16[64,32,512]{2,1,0:T(8,128)(2,1)}), bf16[64,32,512]{2,1,0:T(8,128)(2,1)S(1)}, u32[]{:S(2)}, u32[]{:S(2)}) async-start(bf16[64,32,512]{2,1,0:T(8,128)(2,1)} %bitcast.7), calls=%async_computation.1 | async-start | bytes 4194304 | tf_op jit(solution)/shard_map/all_to_all | solution.py:390
  70.1 0.9 fusion.18.coulomb_ref
  70.9 0.0 copy-done
  71.0 0.0 copy-done.3
  71.0 1.7 fusion.1.weights_ref
  72.7 45.3 %all-to-all-done.1 = bf16[64,32,512]{2,1,0:T(8,128)(2,1)S(1)} async-done(((bf16[64,32,512]{2,1,0:T(8,128)(2,1)}), bf16[64,32,512]{2,1,0:T(8,128)(2,1)S(1)}, u32[]{:S(2)}, u32[]{:S(2)}) %all-to-all-start.1) | async-done | bytes 2097184 | tf_op jit(solution)/shard_map/all_to_all | solution.py:390
  118.0 0.0 copy-start.1
  118.0 0.0 copy-done.2
  118.0 0.0 copy-done.4
  118.0 3.8 %fusion.part_ref = f32[2048,512]{1,0:T(8,128)} fusion(bf16[2048,512]{1,0:T(8,128)(2,1)S(1)} %bitcast.5, bf16[512,512]{1,0:T(8,128)(2,1)S(1)} %copy-done.2, bf16[512,512]{1,0:T(8,128)(2,1)S(1)} %copy-done.4, f32[512]{0:T(512)S(1)} %fusion.40), kind=kOutput, calls=%fused_computation.1 | convolution fusion | flops 1343225856 | bytes 7342080 | tf_op jit(solution)/shard_map/dot_general | solution.py:403
  121.8 0.0 copy-done.1
  121.8 57.3 %sum_projections.1.proj_ref = bf16[4,2048,128]{2,1,0:T(8,128)(2,1)} custom-call(f32[2048,512]{1,0:T(8,128)} %fusion.part_ref), custom_call_target="tpu_custom_call" | custom-call | tf_op jit(solution)/shard_map/sum_projections/pallas_call | solution.py:319
  179.1 15.8 %respond.1 = bf16[8,512,512]{2,1,0:T(8,128)(2,1)} custom-call(bf16[2048,512]{1,0:T(8,128)(2,1)} %bitcast.6, bf16[512,512]{1,0:T(8,128)(2,1)} %constant.82.clone.perm_ref, f32[2048,8]{1,0:T(8,128)} %fusion.1.weights_ref, bf16[4,2048,128]{2,1,0:T(8,128)(2,1)} %sum_projections.1.proj_ref, f32[512,1]{1,0:T(8,128)} %fusion.18.coulomb_ref), custom_call_target="tpu_custom_call" | custom-call | tf_op jit(solution)/shard_map/respond/pallas_call | solution.py:373
  (1 shorter events, 0.0 us)
Async XLA Ops:
  0.0 71.0 %copy-start = (f32[64,8]{0,1:T(8,128)S(1)}, f32[64,8]{0,1:T(8,128)}, u32[]{:S(2)}) copy-start(f32[64,8]{0,1:T(8,128)} %param.18) | copy-start | bytes 6148
  57.3 13.6 %copy-start.3 = (s32[2048]{0:T(1024)S(1)}, s32[2048]{0:T(1024)}, u32[]{:S(2)}) copy-start(s32[2048]{0:T(1024)} %param.17) | copy-start | bytes 24580
  57.3 60.7 %copy-start.2 = (bf16[512,512]{1,0:T(8,128)(2,1)S(1)}, bf16[512,512]{1,0:T(8,128)(2,1)}, u32[]{:S(2)}) copy-start(bf16[512,512]{1,0:T(8,128)(2,1)} %constant.82.clone.perm_ref) | copy-start | bytes 1572868
  57.3 60.7 %copy-start.4 = (bf16[512,512]{1,0:T(8,128)(2,1)S(1)}, bf16[512,512]{1,0:T(8,128)(2,1)}, u32[]{:S(2)}) copy-start(bf16[512,512]{1,0:T(8,128)(2,1)} %param.19) | copy-start | bytes 1572868
  57.3 60.7 %all-to-all-start.1 = ((bf16[64,32,512]{2,1,0:T(8,128)(2,1)}), bf16[64,32,512]{2,1,0:T(8,128)(2,1)S(1)}, u32[]{:S(2)}, u32[]{:S(2)}) async-start(bf16[64,32,512]{2,1,0:T(8,128)(2,1)} %bitcast.7), calls=%async_computation.1 | async-start | bytes 4194304 | tf_op jit(solution)/shard_map/all_to_all | solution.py:390
  118.0 3.8 %copy-start.1 = (bf16[64,32,512]{2,1,0:T(8,128)(2,1)}, bf16[64,32,512]{2,1,0:T(8,128)(2,1)S(1)}, u32[]{:S(2)}) copy-start(bf16[64,32,512]{2,1,0:T(8,128)(2,1)S(1)} %all-to-all-done.1) | copy-start | bytes 6291460

commit v2 on v0

v2 whole, which is shorter than its diff:
```python
import math

import jax
import jax.numpy as jnp
import ml_dtypes
import numpy as np
from jax import lax
from jax.experimental import pallas as pl
from jax.experimental.pallas import tpu as pltpu
from jax.sharding import PartitionSpec as P

GRID = 64
MESH = pl.DeviceIdType.MESH
F32, BF16 = jnp.float32, jnp.bfloat16
LIMIT = 60 * 1024 * 1024


def rounded(values):
    return values.astype(np.float32).astype(ml_dtypes.bfloat16).astype(np.float32)


def tables():
    at = np.arange(GRID)
    half = np.arange(GRID // 2)
    scaling = 1.0 / math.sqrt(GRID)
    step = 2.0 * math.pi / GRID
    z_angles = (at[:, None] * half[None, :] % GRID) * step
    z_real = rounded(scaling * np.cos(z_angles))
    z_imag = rounded(-scaling * np.sin(z_angles))
    signed = np.where(half < GRID // 4, half, half - GRID // 2)
    y_angles = (signed[:, None] * at[None, :] % GRID) * step
    y_cos = rounded(scaling * np.cos(y_angles))
    y_sin = rounded(scaling * np.sin(y_angles))
    x_angles = (at[:, None] * at[None, :] % GRID) * step
    x_cos = rounded(scaling * np.cos(x_angles))
    x_sin = rounded(scaling * np.sin(x_angles))
    zr = z_real.reshape(GRID, 4, 8).transpose(1, 0, 2)
    zi = z_imag.reshape(GRID, 4, 8).transpose(1, 0, 2)

    def spread(first, second):
        both = np.stack([first, second], 2)[:, :, :, None, :]
        return np.broadcast_to(both, (4, GRID, 2, 16, 8)).reshape(4, GRID, 256)

    z_first = spread(zr, zi)
    z_second = spread(zi, -zr)

    def widen(table):
        table = table[:, :32].reshape(16, 2, 32).transpose(1, 2, 0)
        return np.broadcast_to(table[:, :, None, :, None], (2, 32, 2, 16, 8)).reshape(2, 32, 256)

    x_table = np.block([[x_cos, x_sin], [-x_sin, x_cos]])
    perm = np.zeros((512, 512), np.float32)
    parity, part, j16, kz8 = np.meshgrid(np.arange(2), np.arange(2), np.arange(16), np.arange(8), indexing="ij")
    inner = np.arange(512)
    outer = ((2 * j16 + parity) * 16 + 2 * kz8 + part).reshape(-1)
    perm[outer, inner] = 1.0
    small = [z_first, z_second, widen(y_cos), widen(y_sin), x_table, perm, perm.T]
    return [np.ascontiguousarray(t).astype(ml_dtypes.bfloat16) for t in small]


def place():
    wide, narrow = lax.axis_index("wide"), lax.axis_index("narrow")
    z, x_hi, y = wide // 8, wide // 4 % 2, wide % 4
    x_lo, core = narrow // 2, narrow % 2
    return x_hi * 2 + x_lo, y, z, core


def device(x, y, z, core):
    return (z * 8 + x // 2 * 4 + y, x % 2 * 2 + core)


def coulomb_column():
    freq_x, narrow = lax.axis_index("wide"), lax.axis_index("narrow")
    freq_x = jnp.where(freq_x < GRID // 2, freq_x, freq_x - GRID)
    at = lax.broadcasted_iota(jnp.int32, (512, 1), 0)
    freq_y = at >> 4
    freq_y = jnp.where(freq_y < GRID // 4, freq_y, freq_y - GRID // 2)
    freq_z = narrow * 8 + ((at & 15) >> 1)
    squared = (freq_x * freq_x + freq_y * freq_y + freq_z * freq_z).astype(F32)
    quarter = float(GRID // 4)
    return 1.0 / jnp.sqrt(1.0 + squared * (1.0 / (quarter * quarter)))


def tile(start, size, unit=16):
    return pl.ds(pl.multiple_of(start, unit), size)


def main_kernel(
    occ_at, emp_at, occ_ref, emp_ref, z_first, z_second, y_cos, y_sin, x_table, perm_ref, perm_t_ref,
    level_ref, denom_ref, trial_ref,
    turned_ref, weights_ref, out_ref,
    x_scr, w_scr, blocks, gathered, columns_f32, waves, pairs, scaled, core_send, core_recv, acc,
    axis_send, axis_recv, z_send, z_recv, z_all,
    narrow_sent, narrow_got, wide_sent, wide_got, send_sem, recv_sem,
):
    wide, narrow = lax.axis_index("wide"), lax.axis_index("narrow")
    x, y, z, core = place()
    x_lo = narrow // 2
    mate = device(x, y, z, 1 - core)
    axis_mates = (
        [device((x + step) % 4, y, z, core) for step in range(1, 4)],
        [device(x, (y + step) % 4, z, core) for step in range(1, 4)],
    )
    z_mates = [device(x, y, (z + step) % 8, core) for step in range(1, 8)]

    barrier = pltpu.get_barrier_semaphore()

    @pl.loop(1, 64)
    def _(step):
        pl.semaphore_signal(barrier, inc=1, device_id=((wide + step) % 64, narrow), device_id_type=MESH)

    for step in range(1, 4):
        pl.semaphore_signal(barrier, inc=1, device_id=(wide, (narrow + step) % 4), device_id_type=MESH)
    across = device(jnp.where(x_lo == 0, (x + 3) % 4, (x + 1) % 4), y, z, core)
    pl.semaphore_signal(barrier, inc=1, device_id=across, device_id_type=MESH)

    @pl.loop(0, 32)
    def _(pair):
        product = occ_ref[occ_at[pair]].astype(F32) * emp_ref[emp_at[pair]].astype(F32)
        low, high = product[:, :2048], product[:, 2048:]
        rows = tile(pair * 16, 16)
        x_scr[0, rows, :] = (low + high).astype(BF16)
        x_scr[1, rows, :] = (low - high).astype(BF16)

    def narrow_copy(k, half, parity):
        peer = (x_lo + 1 - k // 2) % 2 * 2 + (core + (k + 1) // 2 % 2) % 2
        at = (half * 2 + parity) * 3 + k
        return pltpu.make_async_remote_copy(
            src_ref=blocks.at[k, half, parity], dst_ref=gathered.at[narrow, half, parity],
            send_sem=narrow_sent.at[at], recv_sem=narrow_got.at[at],
            device_id=(wide, peer), device_id_type=MESH,
        )

    for parity in range(2):
        for n in range(4):
            first = z_first[n].astype(F32)
            second = z_second[n].astype(F32)

            @pl.loop(0, 4)
            def _(group):
                cos8 = y_cos[parity, tile(group * 8, 8, 8), :].astype(F32)
                sin8 = y_sin[parity, tile(group * 8, 8, 8), :].astype(F32)
                for inner in range(8):
                    w_scr[n, tile(group * 512 + inner * 64, 64), :] = (
                        first * cos8[inner : inner + 1] + second * sin8[inner : inner + 1]
                    ).astype(BF16)

        if parity == 0:
            pl.semaphore_wait(barrier, 67)

        @pl.loop(0, 4)
        def _(k):
            peer = (x_lo + 1 - k // 2) % 2 * 2 + (core + (k + 1) // 2 % 2) % 2
            plane = jnp.dot(x_scr[parity], w_scr[peer], preferred_element_type=F32).astype(BF16)

            @pl.when(k < 3)
            def _():
                blocks[k, 0, parity] = plane[:256]
                blocks[k, 1, parity] = plane[256:]
                narrow_copy(k, 0, parity).start()

            @pl.when(k == 3)
            def _():
                gathered[narrow, 0, parity] = plane[:256]
                gathered[narrow, 1, parity] = plane[256:]

    for parity in range(2):
        for k in range(3):
            narrow_copy(k, 1, parity).start()

    column = coulomb_column()
    trial = (column * trial_ref[...].astype(F32)).astype(BF16)
    trial = jnp.dot(perm_t_ref[...], trial, preferred_element_type=F32).astype(BF16)
    scaled[0] = jnp.where(core == 0, trial[:, :256], trial[:, 256:])
    scaled[1] = jnp.where(core == 0, trial[:, 256:], trial[:, :256])

    def wide_copy(chunk, peer):
        return pltpu.make_async_remote_copy(
            src_ref=waves.at[chunk, peer], dst_ref=pairs.at[chunk, wide],
            send_sem=wide_sent.at[chunk], recv_sem=wide_got.at[chunk],
            device_id=(peer, narrow), device_id_type=MESH,
        )

    def wide_all(chunk):
        whole = pairs.at[chunk, pl.ds(0, 63)]
        return pltpu.make_async_remote_copy(
            src_ref=whole, dst_ref=whole, send_sem=wide_sent.at[chunk], recv_sem=wide_got.at[chunk],
            device_id=mate, device_id_type=MESH,
        )

    for chunk in range(4):
        half, parity = chunk // 2, chunk % 2
        for k in range(3):
            narrow_copy(k, half, parity).wait_recv()

        @pl.loop(0, 4)
        def _(group):
            stacked = jnp.concatenate(
                [
                    jnp.concatenate(
                        [
                            gathered[n, half, parity, tile(group * 64 + q * 16, 16), part * 128 : part * 128 + 128]
                            for q in range(4)
                        ],
                        1,
                    )
                    for part in range(2)
                    for n in range(4)
                ],
                0,
            )
            result = jnp.dot(x_table[...], stacked, preferred_element_type=F32)
            for q in range(4):
                for part in range(2):
                    columns_f32[part, pl.ds(group * 4 + q, 64, stride=16), :] = result[
                        part * 64 : part * 64 + 64, q * 128 : q * 128 + 128
                    ]

        @pl.loop(0, 8)
        def _(group):
            for part in range(2):
                waves[chunk, tile(group * 8, 8, 8), :, part * 128 : part * 128 + 128] = (
                    columns_f32[part, tile(group * 128, 128), :].astype(BF16).reshape(8, 16, 128)
                )

        @pl.loop(1, 64)
        def _(step):
            wide_copy(chunk, (wide + step) % 64).start()

        pairs[chunk, wide] = waves[chunk, wide]

    table = denom_ref[...]
    onehot = (lax.broadcasted_iota(jnp.int32, (NTAB, 2048), 0) == level_ref[...]).astype(F32).astype(BF16)
    picked = jnp.zeros((2048, 128), F32)
    for _ in range(3):
        piece = table.astype(BF16)
        table = table - piece.astype(F32)
        picked += lax.dot_general(onehot, piece, (((0,), (0,)), ((), ())), preferred_element_type=F32)
    picked = picked.reshape(64, 2, 16, 128)
    for half in range(2):
        weights_ref[half] = picked[:, half].reshape(1024, 128)

    count = [0]
    sent = []

    def send(src, dst, peer):
        at = count[0]
        count[0] += 1
        copy = pltpu.make_async_remote_copy(
            src_ref=src, dst_ref=dst, send_sem=send_sem.at[at], recv_sem=recv_sem.at[at],
            device_id=peer, device_id_type=MESH,
        )
        copy.start()
        sent.append(copy)
        return copy

    def project(half, which, rows):
        return jnp.dot(
            pairs[half * 2, pl.ds(rows, 16)].reshape(256, 256), scaled[which, 0:256],
            preferred_element_type=F32,
        ) + jnp.dot(
            pairs[half * 2 + 1, pl.ds(rows, 16)].reshape(256, 256), scaled[which, 256:512],
            preferred_element_type=F32,
        )

    def turn(half):
        @pl.loop(0, 2)
        def _(piece):
            total = jnp.zeros((512, 512), F32)
            for parity in range(2):
                total += lax.dot_general(
                    perm_ref[:, parity * 256 : parity * 256 + 256],
                    pairs[half * 2 + parity, tile(piece * 32, 32)].reshape(512, 256),
                    (((1,), (1,)), ((), ())),
                    preferred_element_type=F32,
                )
            turned_ref[half * 2 + piece] = total.astype(BF16)

    def reduce(half):
        for parity in range(2):
            wide_all(half * 2 + parity).wait_recv()
        copies = []
        for piece in range(4):
            rows = pl.ds(piece * 256, 256)
            core_send[half, rows, :] = project(half, 1, piece * 16).astype(BF16)
            copies.append(send(core_send.at[half, rows], core_recv.at[half, rows], mate))
        for piece in range(4):
            own = project(half, 0, piece * 16)
            acc[half, 0, piece * 256 : piece * 256 + 256, :] = own[:, :128]
            acc[half, 1, piece * 256 : piece * 256 + 256, :] = own[:, 128:]
        yield
        for piece in range(4):
            rows = pl.ds(piece * 256, 256)
            copies[piece].wait_recv()
            for h in range(2):
                acc[half, h, rows, :] += core_recv[half, rows, h * 128 : h * 128 + 128].astype(F32)
        base = [0, 0]
        places = ((x, y), (y, x))
        for stage in range(2):
            size = 256 if stage == 0 else 64
            copies = {}
            for h in range(2):
                for step in range(1, 4):
                    rows = tile(base[h] + (places[stage][h] + step) % 4 * size, size)
                    axis_send[half, stage, h, step, 0:size] = acc[half, h, rows, :].astype(BF16)
                    copies[h, step] = send(
                        axis_send.at[half, stage, h, step, pl.ds(0, size)],
                        axis_recv.at[half, stage, h, step, pl.ds(0, size)],
                        axis_mates[(h + stage) % 2][step - 1],
                    )
            yield
            for h in range(2):
                for step in range(1, 4):
                    copies[h, step].wait_recv()
                base[h] = base[h] + places[stage][h] * size
                rows = tile(base[h], size)
                total = acc[half, h, rows, :]
                for step in range(1, 4):
                    total += axis_recv[half, stage, h, step, 0:size].astype(F32)
                acc[half, h, rows, :] = total
        copies = []
        for step in range(1, 8):
            for h in range(2):
                z_send[half, step, h] = acc[half, h, tile(base[h] + (z + step) % 8 * 8, 8, 8), :]
            copies.append(send(z_send.at[half, step], z_recv.at[half, step], z_mates[step - 1]))
        yield
        for copy in copies:
            copy.wait_recv()
        for h in range(2):
            total = acc[half, h, tile(base[h] + z * 8, 8, 8), :]
            for step in range(1, 8):
                total += z_recv[half, step, h]
            z_all[half, z, h] = total
        mine = z_all.at[half, z]
        copies = [send(mine, mine, peer) for peer in z_mates]
        yield
        for copy in copies:
            copy.wait_recv()
        for h in range(2):
            out_ref[core * 2 + h, tile(half * 1024 + base[h], 64), :] = (
                z_all[half, :, h].reshape(64, 128).astype(BF16)
            )
        for stage in (1, 0):
            size = 256 if stage == 0 else 64
            copies = {}
            for h in range(2):
                mine = out_ref.at[core * 2 + h, tile(half * 1024 + base[h], size)]
                for step in range(1, 4):
                    copies[h, step] = send(mine, mine, axis_mates[(h + stage) % 2][step - 1])
            last = []
            if stage == 0:
                for h in range(2):
                    mine = out_ref.at[core * 2 + h, tile(half * 1024 + base[h], size)]
                    last.append(send(mine, mine, mate))
            yield
            for step in range(1, 4):
                for h in range(2):
                    copies[h, step].wait_recv()
                    if stage == 0:
                        start = half * 1024 + (places[0][h] + 4 - step) % 4 * 256
                        piece = out_ref.at[core * 2 + h, tile(start, 256)]
                        last.append(send(piece, piece, mate))
            for h in range(2):
                base[h] = base[h] - places[stage][h] * size
        yield
        for copy in last:
            copy.wait_recv()

    runs = [reduce(half) for half in range(2)]
    if LOCKSTEP:
        next(runs[0])
        turn(0)
        next(runs[1])
        turn(1)
        alive = runs
        while alive:
            alive = [run for run in alive if next(run, 1) is None]
    else:
        next(runs[0])
        turn(0)
        for _ in runs[0]:
            pass
        next(runs[1])
        turn(1)
        for _ in runs[1]:
            pass

    for parity in range(2):
        for half in range(2):
            for k in range(3):
                narrow_copy(k, half, parity).wait_send()
    for chunk in range(4):
        wide_all(chunk).wait_send()
    for copy in sent:
        copy.wait_send()


LOCKSTEP = True
NTAB = 64


def main(pair_occ, pair_emp, *arrays):
    smem = pl.BlockSpec(memory_space=pltpu.SMEM)
    vmem = pl.BlockSpec(memory_space=pltpu.VMEM)
    copies = 2 * (4 + 12 + 7 + 7 + 12 + 8)
    dma = pltpu.SemaphoreType.DMA
    return pl.pallas_call(
        main_kernel,
        out_shape=(
            jax.ShapeDtypeStruct((4, 512, 512), BF16),
            jax.ShapeDtypeStruct((2, 1024, 128), F32),
            jax.ShapeDtypeStruct((4, 2048, 128), BF16),
        ),
        in_specs=[smem, smem] + [vmem] * len(arrays),
        out_specs=(vmem, vmem, vmem),
        scratch_shapes=[
            pltpu.VMEM((2, 512, 2048), BF16),
            pltpu.VMEM((4, 2048, 256), BF16),
            pltpu.VMEM((3, 2, 2, 256, 256), BF16),
            pltpu.VMEM((4, 2, 2, 256, 256), BF16),
            pltpu.VMEM((2, 1024, 128), F32),
            pltpu.VMEM((4, 64, 16, 256), BF16),
            pltpu.VMEM((4, 64, 16, 256), BF16),
            pltpu.VMEM((2, 512, 256), BF16),
            pltpu.VMEM((2, 1024, 256), BF16),
            pltpu.VMEM((2, 1024, 256), BF16),
            pltpu.VMEM((2, 2, 1024, 128), F32),
            pltpu.VMEM((2, 2, 2, 4, 256, 128), BF16),
            pltpu.VMEM((2, 2, 2, 4, 256, 128), BF16),
            pltpu.VMEM((2, 8, 2, 8, 128), F32),
            pltpu.VMEM((2, 8, 2, 8, 128), F32),
            pltpu.VMEM((2, 8, 2, 8, 128), F32),
            dma((12,)), dma((12,)), dma((4,)), dma((4,)), dma((copies,)), dma((copies,)),
        ],
        compiler_params=pltpu.CompilerParams(vmem_limit_bytes=LIMIT, collective_id=0, has_side_effects=True),
        name="main",
    )(pair_occ, pair_emp, *arrays)


def response_kernel(turned_ref, weights_ref, proj_ref, out_ref):
    w = pl.program_id(0)
    total = jnp.zeros((512, 512), F32)
    for piece in range(8):
        rows = slice(piece * 256, piece * 256 + 256)
        weights = weights_ref[rows, :]
        column = pltpu.roll(weights, (128 - w) % 128, 1)[:, 0:1]
        weighted = jnp.concatenate(
            [(proj_ref[block, rows, :].astype(F32) * column).astype(BF16) for block in range(4)], 1
        )
        at = piece % 2 * 256
        total += jnp.dot(turned_ref[piece // 2, :, at : at + 256], weighted, preferred_element_type=F32)
    out_ref[0] = (total * coulomb_column()).astype(BF16)


def respond(turned, weights, projections):
    def whole(*shape):
        return pl.BlockSpec(shape, lambda w: (0,) * len(shape))

    return pl.pallas_call(
        response_kernel,
        out_shape=jax.ShapeDtypeStruct((8, 512, 512), BF16),
        grid=(8,),
        in_specs=[whole(4, 512, 512), whole(2048, 128), whole(4, 2048, 128)],
        out_specs=pl.BlockSpec((1, 512, 512), lambda w: (w, 0, 0)),
        compiler_params=pltpu.CompilerParams(vmem_limit_bytes=LIMIT),
        name="respond",
    )(turned, weights, projections)


def shards(occupied, empty, pair_occ, pair_emp, pair_level, denominators, trial):
    constants = [jnp.asarray(t) for t in tables()]
    turned, weights, projections = main(
        pair_occ, pair_emp, occupied, empty, *constants,
        pair_level.reshape(1, 2048), jnp.pad(denominators, ((0, 0), (0, 120))), trial,
    )
    return respond(turned, weights.reshape(2048, 128), projections)


def solution(mesh):
    placed = (
        P("wide", "narrow", None),
        P("wide", "narrow", None),
        P("wide"),
        P("wide"),
        P(),
        P(),
        P(("wide", "narrow"), None),
    )
    return jax.shard_map(
        shards,
        mesh=mesh,
        in_specs=placed,
        out_specs=P(None, ("wide", "narrow"), None),
        check_vma=False,
    )
```

time: 589 us -> 133 us (0.23); the launches traced: 582 us -> 133 us
  waiting for transfers between devices: 339 us -> 0 us
  Pallas kernels: 0 us -> 131 us
  local copies, waits for them, and re-layouts: 119 us -> 1.39 us
  other arithmetic: 45.5 us -> 0 us
  matrix products: 45.3 us -> 0 us
  starting transfers between devices: 19.4 us -> 0 us
  between operations: 13.7 us -> 0.01 us
    psum x1 -> x0, waiting for transfers between devices: 266 us -> none  [shards(): projections = lax.psum(partial_term, ('wide', 'narrow'))]
    pallas_call x0 -> x2, Pallas kernels: none -> 131 us  [the longest x1 116 us: main(): pl.pallas_call(main_kernel, out_shape=(jax.ShapeDtypeStruct((4, 512, 512)...]
    all_to_all x2 -> x0, waiting for transfers between devices: 72.6 us -> none  [the longest x1 48 us: shards(): lax.all_to_all(pair_waves, 'wide', split_axis=1, concat_axis=0, tiled=True)]
    dot_general x5 -> x0, matrix products: 45.3 us -> none  [the longest x1 17.1 us: shards(): jnp.einsum('skx,pxyq->spkyq', x_table, gathered, preferred_element_type=j...]
    convert_element_type x5 -> x0, local copies, waits for them, and re-layouts: 35 us -> none  [the longest x1 12.6 us: shards(): (occ_rows.astype(jnp.float32) * emp_rows.astype(jnp.float32)).astype(jnp....]
    transpose x1 -> x0, local copies, waits for them, and re-layouts: 24.2 us -> none  [shards(): jnp.einsum('sky,pxyq->spxkq', y_table, along_z, preferred_element_type=jn...]
    add x2 -> x0, other arithmetic: 22.3 us -> none  [combine_parts(): real_part = halves[0, ..., 0] + halves[1, ..., 1]]
    all_to_all x2 -> x0, starting transfers between devices: 19.3 us -> none  [the longest x1 12.6 us: shards(): lax.all_to_all(pair_waves, 'wide', split_axis=1, concat_axis=0, tiled=True)]
  transfers between devices with their start and end apart: 3 -> 0, of which waited for: 3 -> 0; matrix products, arithmetic and copies ran while one was open for 0% -> 0% of each run, Pallas kernels for 0% -> 0%
where the time goes in v2:
time: 133 us
  Pallas kernels  131 us (98%)
  local copies, waits for them, and re-layouts  1.39 us (1%)
    pallas_call x1, Pallas kernels, main(): pl.pallas_call(main_kernel, out_shape=(jax.ShapeDtypeStruct((4, 512, 512)...  116 us
    pallas_call x1, Pallas kernels, respond(): pl.pallas_call(response_kernel, out_shape=jax.ShapeDtypeStruct((8, 512, 5...  15.4 us

profile of v2, /device:TPU:1, one launch (start us, length us, event | category | flops | bytes accessed | tf_op | source)
XLA Modules:
  0.0 132.9 jit_solution(4123623974366349369)
XLA Ops:
  0.0 0.8 copy.15
  0.8 0.6 pad.4.denom_ref
  1.4 116.1 %main.1 = (bf16[4,512,512]{2,1,0:T(8,128)(2,1)}, f32[2,1024,128]{2,1,0:T(8,128)}, bf16[4,2048,128]{2,1,0:T(8,128)(2,1)}) custom-call(s32[32]{0:T(128)} %occ_at.1, s32[32]{0:T(128)} %emp_at.1, bf16[8,16,4096]{2,1,0:T(8,128)(2,1)} %occ_ref.1, bf16[16,16,4096]{2,1,0:T(8,128)(2,1)} %emp_ref.1, bf16[4,64,256]{2,1,0:T(8,128)(2,1)} %constant.17.clone.z_first, ...), custom_call_target="tpu_custom_call" | custom-call | tf_op jit(solution)/shard_map/main/pallas_call | solution.py:407
  117.5 15.4 %respond.1 = bf16[8,512,512]{2,1,0:T(8,128)(2,1)} custom-call(bf16[4,512,512]{2,1,0:T(8,128)(2,1)} %get-tuple-element.8.turned_ref, f32[2048,128]{1,0:T(8,128)} %bitcast.2, bf16[4,2048,128]{2,1,0:T(8,128)(2,1)} %get-tuple-element.10.proj_ref), custom_call_target="tpu_custom_call" | custom-call | tf_op jit(solution)/shard_map/respond/pallas_call | solution.py:459

commit v3 on v2

--- a/solution.py
+++ b/solution.py
@@ -12,7 +12,8 @@
 GRID = 64
 MESH = pl.DeviceIdType.MESH
 F32, BF16 = jnp.float32, jnp.bfloat16
-LIMIT = 60 * 1024 * 1024
+MAIN_LIMIT = 62 * 1024 * 1024
+RESPOND_LIMIT = 60 * 1024 * 1024
 
 
 def rounded(values):
@@ -85,11 +86,18 @@
     return pl.ds(pl.multiple_of(start, unit), size)
 
 
+def weigh(w, weights_ref, proj_ref):
+    column = pltpu.roll(weights_ref[0], (128 - w) % 128, 1)[:, 0:1]
+    return jnp.concatenate(
+        [(proj_ref[block, 0:1024].astype(F32) * column).astype(BF16) for block in range(4)], 1
+    )
+
+
 def main_kernel(
-    occ_at, emp_at, occ_ref, emp_ref, z_first, z_second, y_cos, y_sin, x_table, perm_ref, perm_t_ref,
-    level_ref, denom_ref, trial_ref,
-    turned_ref, weights_ref, out_ref,
-    x_scr, w_scr, blocks, gathered, columns_f32, waves, pairs, scaled, core_send, core_recv, acc,
+    occ_at, emp_at, occ_ref, emp_ref, z_first, z_second, y_cos, y_sin, x_table, perm_hbm, perm_t_hbm,
+    level_ref, denom_ref, trial_hbm,
+    turned_ref, weights_ref, out_ref, early_hbm, early, early_sem,
+    trial_ref, perm_ref, perm_t_ref, late_sem, x_scr, w_scr, blocks, gathered, columns_f32, waves, pairs, scaled, core_send, core_recv, acc,
     axis_send, axis_recv, z_send, z_recv, z_all,
     narrow_sent, narrow_got, wide_sent, wide_got, send_sem, recv_sem,
 ):
@@ -114,13 +122,21 @@
     across = device(jnp.where(x_lo == 0, (x + 3) % 4, (x + 1) % 4), y, z, core)
     pl.semaphore_signal(barrier, inc=1, device_id=across, device_id_type=MESH)
 
-    @pl.loop(0, 32)
-    def _(pair):
-        product = occ_ref[occ_at[pair]].astype(F32) * emp_ref[emp_at[pair]].astype(F32)
-        low, high = product[:, :2048], product[:, 2048:]
-        rows = tile(pair * 16, 16)
-        x_scr[0, rows, :] = (low + high).astype(BF16)
-        x_scr[1, rows, :] = (low - high).astype(BF16)
+    late = [
+        pltpu.make_async_copy(src, dst, late_sem.at[at])
+        for at, (src, dst) in enumerate(((trial_hbm, trial_ref), (perm_hbm, perm_ref), (perm_t_hbm, perm_t_ref)))
+    ]
+    for copy in late:
+        copy.start()
+
+    def products(half):
+        @pl.loop(half * 16, half * 16 + 16)
+        def _(pair):
+            product = occ_ref[occ_at[pair]] * emp_ref[emp_at[pair]]
+            low, high = product[:, :2048], product[:, 2048:]
+            rows = tile(pair * 16, 16)
+            x_scr[0, rows, :] = low + high
+            x_scr[1, rows, :] = low - high
 
     def narrow_copy(k, half, parity):
         peer = (x_lo + 1 - k // 2) % 2 * 2 + (core + (k + 1) // 2 % 2) % 2
@@ -131,48 +147,37 @@
             device_id=(wide, peer), device_id_type=MESH,
         )
 
-    for parity in range(2):
-        for n in range(4):
-            first = z_first[n].astype(F32)
-            second = z_second[n].astype(F32)
-
-            @pl.loop(0, 4)
-            def _(group):
-                cos8 = y_cos[parity, tile(group * 8, 8, 8), :].astype(F32)
-                sin8 = y_sin[parity, tile(group * 8, 8, 8), :].astype(F32)
-                for inner in range(8):
-                    w_scr[n, tile(group * 512 + inner * 64, 64), :] = (
-                        first * cos8[inner : inner + 1] + second * sin8[inner : inner + 1]
-                    ).astype(BF16)
-
-        if parity == 0:
-            pl.semaphore_wait(barrier, 67)
-
+    def make_table(parity, n):
+        first = z_first[n]
+        second = z_second[n]
+
+        @pl.loop(0, 2)
+        def _(group):
+            cos8 = y_cos[parity, tile(group * 16, 16), :]
+            sin8 = y_sin[parity, tile(group * 16, 16), :]
+            for inner in range(16):
+                w_scr[parity * 4 + n, tile(group * 1024 + inner * 64, 64), :] = (
+                    first * cos8[inner : inner + 1] + second * sin8[inner : inner + 1]
+                )
+
+    def planes(half, parity):
         @pl.loop(0, 4)
         def _(k):
             peer = (x_lo + 1 - k // 2) % 2 * 2 + (core + (k + 1) // 2 % 2) % 2
-            plane = jnp.dot(x_scr[parity], w_scr[peer], preferred_element_type=F32).astype(BF16)
+            if half == 0:
+                make_table(parity, peer)
+            plane = jnp.dot(
+                x_scr[parity, half * 256 : half * 256 + 256], w_scr[parity * 4 + peer], preferred_element_type=F32
+            ).astype(BF16)
 
             @pl.when(k < 3)
             def _():
-                blocks[k, 0, parity] = plane[:256]
-                blocks[k, 1, parity] = plane[256:]
-                narrow_copy(k, 0, parity).start()
+                blocks[k, half, parity] = plane
+                narrow_copy(k, half, parity).start()
 
             @pl.when(k == 3)
             def _():
-                gathered[narrow, 0, parity] = plane[:256]
-                gathered[narrow, 1, parity] = plane[256:]
-
-    for parity in range(2):
-        for k in range(3):
-            narrow_copy(k, 1, parity).start()
-
-    column = coulomb_column()
-    trial = (column * trial_ref[...].astype(F32)).astype(BF16)
-    trial = jnp.dot(perm_t_ref[...], trial, preferred_element_type=F32).astype(BF16)
-    scaled[0] = jnp.where(core == 0, trial[:, :256], trial[:, 256:])
-    scaled[1] = jnp.where(core == 0, trial[:, 256:], trial[:, :256])
+                gathered[narrow, half, parity] = plane
 
     def wide_copy(chunk, peer):
         return pltpu.make_async_remote_copy(
@@ -188,7 +193,7 @@
             device_id=mate, device_id_type=MESH,
         )
 
-    for chunk in range(4):
+    def along_x(chunk):
         half, parity = chunk // 2, chunk % 2
         for k in range(3):
             narrow_copy(k, half, parity).wait_recv()
@@ -223,18 +228,41 @@
                     columns_f32[part, tile(group * 128, 128), :].astype(BF16).reshape(8, 16, 128)
                 )
 
-        @pl.loop(1, 64)
+        @pl.loop(1, 64, unroll=7)
         def _(step):
-            wide_copy(chunk, (wide + step) % 64).start()
+            wide_copy(chunk, jnp.bitwise_and(wide + step, 63)).start()
 
         pairs[chunk, wide] = waves[chunk, wide]
 
+    products(0)
+    pl.semaphore_wait(barrier, 67)
+    planes(0, 0)
+    planes(0, 1)
+    products(1)
+    planes(1, 0)
+    planes(1, 1)
+    for chunk in range(4):
+        along_x(chunk)
+
+    for copy in late:
+        copy.wait()
+    column = coulomb_column()
+    trial = (column * trial_ref[...].astype(F32)).astype(BF16)
+    trial = jnp.dot(perm_t_ref[...], trial, preferred_element_type=F32).astype(BF16)
+    scaled[0] = jnp.where(core == 0, trial[:, :256], trial[:, 256:])
+    scaled[1] = jnp.where(core == 0, trial[:, 256:], trial[:, :256])
+
     table = denom_ref[...]
-    onehot = (lax.broadcasted_iota(jnp.int32, (NTAB, 2048), 0) == level_ref[...]).astype(F32).astype(BF16)
+    lanes = lax.broadcasted_iota(jnp.int32, (8, 128), 1)
+    spread = (lax.broadcasted_iota(jnp.int32, (8, 128), 0) == lanes).astype(F32).astype(BF16)
+    onehot = (lax.broadcasted_iota(jnp.int32, (NTAB, 2048), 0) == level_ref[...].reshape(1, 2048)).astype(F32).astype(BF16)
     picked = jnp.zeros((2048, 128), F32)
     for _ in range(3):
         piece = table.astype(BF16)
         table = table - piece.astype(F32)
+        piece = lax.dot_general(
+            piece, spread, (((0,), (0,)), ((), ())), preferred_element_type=F32
+        ).astype(BF16)
         picked += lax.dot_general(onehot, piece, (((0,), (0,)), ((), ())), preferred_element_type=F32)
     picked = picked.reshape(64, 2, 16, 128)
     for half in range(2):
@@ -274,7 +302,7 @@
                     (((1,), (1,)), ((), ())),
                     preferred_element_type=F32,
                 )
-            turned_ref[half * 2 + piece] = total.astype(BF16)
+            turned_ref[half, :, tile(piece * 512, 512, 512)] = total.astype(BF16)
 
     def reduce(half):
         for parity in range(2):
@@ -367,23 +395,36 @@
             copy.wait_recv()
 
     runs = [reduce(half) for half in range(2)]
-    if LOCKSTEP:
+    def response_copy(w):
+        return pltpu.make_async_copy(early.at[w], early_hbm.at[w], early_sem.at[w])
+
+    def respond_early(first, last):
+        @pl.loop(first, last)
+        def _(w):
+            weighted = weigh(w, weights_ref, out_ref)
+            early[w] = jnp.dot(turned_ref[0], weighted, preferred_element_type=F32).astype(BF16)
+            response_copy(w).start()
+
+    next(runs[0])
+    turn(0)
+    for _ in range(3):
         next(runs[0])
-        turn(0)
+    next(runs[1])
+    turn(1)
+    for _ in range(4):
+        next(runs[0])
         next(runs[1])
-        turn(1)
-        alive = runs
-        while alive:
-            alive = [run for run in alive if next(run, 1) is None]
-    else:
-        next(runs[0])
-        turn(0)
-        for _ in runs[0]:
-            pass
-        next(runs[1])
-        turn(1)
-        for _ in runs[1]:
-            pass
+    for _ in runs[0]:
+        pass
+    respond_early(0, 3)
+    next(runs[1])
+    respond_early(3, 5)
+    next(runs[1])
+    respond_early(5, 8)
+    for _ in runs[1]:
+        pass
+    for w in range(8):
+        response_copy(w).wait()
 
     for parity in range(2):
         for half in range(2):
@@ -395,27 +436,34 @@
         copy.wait_send()
 
 
-LOCKSTEP = True
 NTAB = 64
 
 
 def main(pair_occ, pair_emp, *arrays):
     smem = pl.BlockSpec(memory_space=pltpu.SMEM)
     vmem = pl.BlockSpec(memory_space=pltpu.VMEM)
+    hbm = pl.BlockSpec(memory_space=pl.ANY)
     copies = 2 * (4 + 12 + 7 + 7 + 12 + 8)
     dma = pltpu.SemaphoreType.DMA
     return pl.pallas_call(
         main_kernel,
         out_shape=(
-            jax.ShapeDtypeStruct((4, 512, 512), BF16),
+            jax.ShapeDtypeStruct((2, 512, 1024), BF16),
             jax.ShapeDtypeStruct((2, 1024, 128), F32),
             jax.ShapeDtypeStruct((4, 2048, 128), BF16),
+            jax.ShapeDtypeStruct((8, 512, 512), BF16),
         ),
-        in_specs=[smem, smem] + [vmem] * len(arrays),
-        out_specs=(vmem, vmem, vmem),
+        in_specs=[smem, smem] + [vmem] * 7 + [hbm] * 2 + [vmem] * 2 + [hbm],
+        out_specs=(vmem, vmem, vmem, hbm),
         scratch_shapes=[
+            pltpu.VMEM((8, 512, 512), BF16),
+            dma((8,)),
+            pltpu.VMEM((512, 512), BF16),
+            pltpu.VMEM((512, 512), BF16),
+            pltpu.VMEM((512, 512), BF16),
+            dma((3,)),
             pltpu.VMEM((2, 512, 2048), BF16),
-            pltpu.VMEM((4, 2048, 256), BF16),
+            pltpu.VMEM((8, 2048, 256), BF16),
             pltpu.VMEM((3, 2, 2, 256, 256), BF16),
             pltpu.VMEM((4, 2, 2, 256, 256), BF16),
             pltpu.VMEM((2, 1024, 128), F32),
@@ -432,48 +480,50 @@
             pltpu.VMEM((2, 8, 2, 8, 128), F32),
             dma((12,)), dma((12,)), dma((4,)), dma((4,)), dma((copies,)), dma((copies,)),
         ],
-        compiler_params=pltpu.CompilerParams(vmem_limit_bytes=LIMIT, collective_id=0, has_side_effects=True),
+        compiler_params=pltpu.CompilerParams(vmem_limit_bytes=MAIN_LIMIT, collective_id=0, has_side_effects=True),
         name="main",
     )(pair_occ, pair_emp, *arrays)
 
 
-def response_kernel(turned_ref, weights_ref, proj_ref, out_ref):
-    w = pl.program_id(0)
-    total = jnp.zeros((512, 512), F32)
-    for piece in range(8):
-        rows = slice(piece * 256, piece * 256 + 256)
-        weights = weights_ref[rows, :]
-        column = pltpu.roll(weights, (128 - w) % 128, 1)[:, 0:1]
-        weighted = jnp.concatenate(
-            [(proj_ref[block, rows, :].astype(F32) * column).astype(BF16) for block in range(4)], 1
-        )
-        at = piece % 2 * 256
-        total += jnp.dot(turned_ref[piece // 2, :, at : at + 256], weighted, preferred_element_type=F32)
-    out_ref[0] = (total * coulomb_column()).astype(BF16)
-
-
-def respond(turned, weights, projections):
-    def whole(*shape):
-        return pl.BlockSpec(shape, lambda w: (0,) * len(shape))
-
+def response_kernel(early_ref, turned_ref, weights_ref, proj_ref, out_ref, even, odd):
+    step = pl.program_id(0)
+    column = coulomb_column()
+
+    @pl.when(step == 0)
+    def _():
+        even[...] = weigh(0, weights_ref, proj_ref)
+
+    for at, (now, later) in enumerate(((even, odd), (odd, even))):
+        total = early_ref[at].astype(F32) + jnp.dot(turned_ref[0], now[...], preferred_element_type=F32)
+        later[...] = weigh(step * 2 + at + 1, weights_ref, proj_ref)
+        out_ref[at] = (total * column).astype(BF16)
+
+
+def respond(early, turned, weights, projections):
     return pl.pallas_call(
         response_kernel,
         out_shape=jax.ShapeDtypeStruct((8, 512, 512), BF16),
-        grid=(8,),
-        in_specs=[whole(4, 512, 512), whole(2048, 128), whole(4, 2048, 128)],
-        out_specs=pl.BlockSpec((1, 512, 512), lambda w: (w, 0, 0)),
-        compiler_params=pltpu.CompilerParams(vmem_limit_bytes=LIMIT),
+        grid=(4,),
+        in_specs=[
+            pl.BlockSpec((2, 512, 512), lambda w: (w, 0, 0)),
+            pl.BlockSpec((1, 512, 1024), lambda w: (1, 0, 0)),
+            pl.BlockSpec((1, 1024, 128), lambda w: (1, 0, 0)),
+            pl.BlockSpec((4, 1024, 128), lambda w: (0, 1, 0)),
+        ],
+        out_specs=pl.BlockSpec((2, 512, 512), lambda w: (w, 0, 0)),
+        scratch_shapes=[pltpu.VMEM((1024, 512), BF16), pltpu.VMEM((1024, 512), BF16)],
+        compiler_params=pltpu.CompilerParams(vmem_limit_bytes=RESPOND_LIMIT),
         name="respond",
-    )(turned, weights, projections)
+    )(early, turned, weights, projections)
 
 
 def shards(occupied, empty, pair_occ, pair_emp, pair_level, denominators, trial):
     constants = [jnp.asarray(t) for t in tables()]
-    turned, weights, projections = main(
+    turned, weights, projections, early = main(
         pair_occ, pair_emp, occupied, empty, *constants,
-        pair_level.reshape(1, 2048), jnp.pad(denominators, ((0, 0), (0, 120))), trial,
+        pair_level, denominators.T, trial,
     )
-    return respond(turned, weights.reshape(2048, 128), projections)
+    return respond(early, turned, weights, projections)
 
 
 def solution(mesh):

time: 133 us -> 124 us (0.932)
  Pallas kernels: 131 us -> 124 us
  local copies, waits for them, and re-layouts: 1.39 us -> 0 us
    pallas_call x1, Pallas kernels: 15.4 us -> 10.5 us  [respond(): pl.pallas_call(response_kernel, out_shape=jax.ShapeDtypeStruct((8, 512, 5...]
    pallas_call x1, Pallas kernels: 116 us -> 113 us  [main(): pl.pallas_call(main_kernel, out_shape=(jax.ShapeDtypeStruct((2, 512, 1024...]
where the time goes in v3:
time: 124 us
  Pallas kernels  124 us (100%)
    pallas_call x1, Pallas kernels, main(): pl.pallas_call(main_kernel, out_shape=(jax.ShapeDtypeStruct((2, 512, 1024...  113 us
    pallas_call x1, Pallas kernels, respond(): pl.pallas_call(response_kernel, out_shape=jax.ShapeDtypeStruct((8, 512, 5...  10.5 us

profile of v3, /device:TPU:1, one launch (start us, length us, event | category | flops | bytes accessed | tf_op | source)
XLA Modules:
  0.0 123.5 jit_solution(6989084437389433489)
XLA Ops:
  0.0 113.0 %main.1 = (bf16[2,512,1024]{2,1,0:T(8,128)(2,1)}, f32[2,1024,128]{2,1,0:T(8,128)}, bf16[4,2048,128]{2,1,0:T(8,128)(2,1)}, bf16[8,512,512]{2,1,0:T(8,128)(2,1)}) custom-call(s32[32]{0:T(128)} %occ_at.1, s32[32]{0:T(128)} %emp_at.1, bf16[8,16,4096]{2,1,0:T(8,128)(2,1)} %occ_ref.1, bf16[16,16,4096]{2,1,0:T(8,128)(2,1)} %emp_ref.1, ...), custom_call_target="tpu_custom_call" | custom-call | tf_op jit(solution)/shard_map/main/pallas_call | solution.py:448
  113.0 10.5 %respond.1 = bf16[8,512,512]{2,1,0:T(8,128)(2,1)} custom-call(bf16[8,512,512]{2,1,0:T(8,128)(2,1)} %get-tuple-element.9.early_ref, bf16[2,512,1024]{2,1,0:T(8,128)(2,1)} %get-tuple-element.10.turned_ref, f32[2,1024,128]{2,1,0:T(8,128)} %get-tuple-element.11.weights_ref, bf16[4,2048,128]{2,1,0:T(8,128)(2,1)} %get-tuple-element.12.proj_ref), custom_call_target="tpu_custom_call" | custom-call | tf_op jit(solution)/shard_map/respond/pallas_call | solution.py:503

commit v4 on v3

--- a/solution.py
+++ b/solution.py
@@ -86,18 +86,19 @@
     return pl.ds(pl.multiple_of(start, unit), size)
 
 
-def weigh(w, weights_ref, proj_ref):
+def weigh(w, weights_ref, proj_ref, blocks):
     column = pltpu.roll(weights_ref[0], (128 - w) % 128, 1)[:, 0:1]
     return jnp.concatenate(
-        [(proj_ref[block, 0:1024].astype(F32) * column).astype(BF16) for block in range(4)], 1
+        [(proj_ref[block, 0:1024].astype(F32) * column).astype(BF16) for block in blocks], 1
     )
 
 
 def main_kernel(
-    occ_at, emp_at, occ_ref, emp_ref, z_first, z_second, y_cos, y_sin, x_table, perm_hbm, perm_t_hbm,
-    level_ref, denom_ref, trial_hbm,
-    turned_ref, weights_ref, out_ref, early_hbm, early, early_sem,
-    trial_ref, perm_ref, perm_t_ref, late_sem, x_scr, w_scr, blocks, gathered, columns_f32, waves, pairs, scaled, core_send, core_recv, acc,
+    occ_at, emp_at, occ_hbm, emp_hbm, z_first_hbm, z_second_hbm, y_cos_hbm, y_sin_hbm, x_table_hbm, perm_hbm, perm_t_hbm,
+    level_hbm, denom_hbm, trial_hbm,
+    turned_ref, weights_ref, out_ref, coulomb_ref, early_hbm, early, early_sem,
+    occ_ref, emp_ref, z_first, z_second, y_cos, y_sin, x_table, perm_ref, perm_t_ref, level_ref, denom_ref, trial_ref,
+    load_sem, x_scr, w_scr, blocks, gathered, columns_f32, waves, pairs, scaled, core_send, core_recv, acc,
     axis_send, axis_recv, z_send, z_recv, z_all,
     narrow_sent, narrow_got, wide_sent, wide_got, send_sem, recv_sem,
 ):
@@ -111,6 +112,19 @@
     )
     z_mates = [device(x, y, (z + step) % 8, core) for step in range(1, 8)]
 
+    loads = [
+        pltpu.make_async_copy(src, dst, load_sem.at[at])
+        for at, (src, dst) in enumerate(
+            (
+                (occ_hbm, occ_ref), (emp_hbm, emp_ref), (z_first_hbm, z_first), (z_second_hbm, z_second),
+                (y_cos_hbm, y_cos), (y_sin_hbm, y_sin), (x_table_hbm, x_table), (perm_hbm, perm_ref),
+                (perm_t_hbm, perm_t_ref), (level_hbm, level_ref), (denom_hbm, denom_ref), (trial_hbm, trial_ref),
+            )
+        )
+    ]
+    for copy in loads:
+        copy.start()
+
     barrier = pltpu.get_barrier_semaphore()
 
     @pl.loop(1, 64)
@@ -121,13 +135,6 @@
         pl.semaphore_signal(barrier, inc=1, device_id=(wide, (narrow + step) % 4), device_id_type=MESH)
     across = device(jnp.where(x_lo == 0, (x + 3) % 4, (x + 1) % 4), y, z, core)
     pl.semaphore_signal(barrier, inc=1, device_id=across, device_id_type=MESH)
-
-    late = [
-        pltpu.make_async_copy(src, dst, late_sem.at[at])
-        for at, (src, dst) in enumerate(((trial_hbm, trial_ref), (perm_hbm, perm_ref), (perm_t_hbm, perm_t_ref)))
-    ]
-    for copy in late:
-        copy.start()
 
     def products(half):
         @pl.loop(half * 16, half * 16 + 16)
@@ -234,19 +241,23 @@
 
         pairs[chunk, wide] = waves[chunk, wide]
 
+    for copy in loads[:7]:
+        copy.wait()
     products(0)
     pl.semaphore_wait(barrier, 67)
     planes(0, 0)
     planes(0, 1)
     products(1)
+    along_x(0)
     planes(1, 0)
     planes(1, 1)
-    for chunk in range(4):
+    for chunk in range(1, 4):
         along_x(chunk)
 
-    for copy in late:
+    for copy in loads[7:]:
         copy.wait()
     column = coulomb_column()
+    coulomb_ref[...] = jnp.broadcast_to(column, (512, 128))
     trial = (column * trial_ref[...].astype(F32)).astype(BF16)
     trial = jnp.dot(perm_t_ref[...], trial, preferred_element_type=F32).astype(BF16)
     scaled[0] = jnp.where(core == 0, trial[:, :256], trial[:, 256:])
@@ -401,7 +412,7 @@
     def respond_early(first, last):
         @pl.loop(first, last)
         def _(w):
-            weighted = weigh(w, weights_ref, out_ref)
+            weighted = weigh(w, weights_ref, out_ref, range(4))
             early[w] = jnp.dot(turned_ref[0], weighted, preferred_element_type=F32).astype(BF16)
             response_copy(w).start()
 
@@ -410,10 +421,11 @@
     for _ in range(3):
         next(runs[0])
     next(runs[1])
-    turn(1)
-    for _ in range(4):
+    for at in range(4):
         next(runs[0])
         next(runs[1])
+        if at == 1:
+            turn(1)
     for _ in runs[0]:
         pass
     respond_early(0, 3)
@@ -451,17 +463,16 @@
             jax.ShapeDtypeStruct((2, 512, 1024), BF16),
             jax.ShapeDtypeStruct((2, 1024, 128), F32),
             jax.ShapeDtypeStruct((4, 2048, 128), BF16),
+            jax.ShapeDtypeStruct((512, 128), F32),
             jax.ShapeDtypeStruct((8, 512, 512), BF16),
         ),
-        in_specs=[smem, smem] + [vmem] * 7 + [hbm] * 2 + [vmem] * 2 + [hbm],
-        out_specs=(vmem, vmem, vmem, hbm),
+        in_specs=[smem, smem] + [hbm] * 12,
+        out_specs=(vmem, vmem, vmem, vmem, hbm),
         scratch_shapes=[
             pltpu.VMEM((8, 512, 512), BF16),
             dma((8,)),
-            pltpu.VMEM((512, 512), BF16),
-            pltpu.VMEM((512, 512), BF16),
-            pltpu.VMEM((512, 512), BF16),
-            dma((3,)),
+            *[pltpu.VMEM(array.shape, array.dtype) for array in arrays],
+            dma((12,)),
             pltpu.VMEM((2, 512, 2048), BF16),
             pltpu.VMEM((8, 2048, 256), BF16),
             pltpu.VMEM((3, 2, 2, 256, 256), BF16),
@@ -485,21 +496,23 @@
     )(pair_occ, pair_emp, *arrays)
 
 
-def response_kernel(early_ref, turned_ref, weights_ref, proj_ref, out_ref, even, odd):
+def response_kernel(early_ref, turned_ref, weights_ref, proj_ref, coulomb_ref, out_ref, even, odd):
     step = pl.program_id(0)
-    column = coulomb_column()
 
     @pl.when(step == 0)
     def _():
-        even[...] = weigh(0, weights_ref, proj_ref)
-
+        even[...] = weigh(0, weights_ref, proj_ref, range(4))
+
+    column = jnp.concatenate([coulomb_ref[...]] * 2, 1)
     for at, (now, later) in enumerate(((even, odd), (odd, even))):
-        total = early_ref[at].astype(F32) + jnp.dot(turned_ref[0], now[...], preferred_element_type=F32)
-        later[...] = weigh(step * 2 + at + 1, weights_ref, proj_ref)
-        out_ref[at] = (total * column).astype(BF16)
-
-
-def respond(early, turned, weights, projections):
+        for lanes in range(2):
+            span = slice(lanes * 256, lanes * 256 + 256)
+            total = jnp.dot(turned_ref[0], now[:, span], preferred_element_type=F32)
+            later[:, span] = weigh(step * 2 + at + 1, weights_ref, proj_ref, range(lanes * 2, lanes * 2 + 2))
+            out_ref[at, :, span] = ((early_ref[at, :, span].astype(F32) + total) * column).astype(BF16)
+
+
+def respond(early, turned, weights, projections, coulomb):
     return pl.pallas_call(
         response_kernel,
         out_shape=jax.ShapeDtypeStruct((8, 512, 512), BF16),
@@ -509,21 +522,22 @@
             pl.BlockSpec((1, 512, 1024), lambda w: (1, 0, 0)),
             pl.BlockSpec((1, 1024, 128), lambda w: (1, 0, 0)),
             pl.BlockSpec((4, 1024, 128), lambda w: (0, 1, 0)),
+            pl.BlockSpec((512, 128), lambda w: (0, 0)),
         ],
         out_specs=pl.BlockSpec((2, 512, 512), lambda w: (w, 0, 0)),
         scratch_shapes=[pltpu.VMEM((1024, 512), BF16), pltpu.VMEM((1024, 512), BF16)],
         compiler_params=pltpu.CompilerParams(vmem_limit_bytes=RESPOND_LIMIT),
         name="respond",
-    )(early, turned, weights, projections)
+    )(early, turned, weights, projections, coulomb)
 
 
 def shards(occupied, empty, pair_occ, pair_emp, pair_level, denominators, trial):
     constants = [jnp.asarray(t) for t in tables()]
-    turned, weights, projections, early = main(
+    turned, weights, projections, coulomb, early = main(
         pair_occ, pair_emp, occupied, empty, *constants,
         pair_level, denominators.T, trial,
     )
-    return respond(early, turned, weights, projections)
+    return respond(early, turned, weights, projections, coulomb)
 
 
 def solution(mesh):

time: 124 us -> 121 us (0.976)
  Pallas kernels: 124 us -> 120 us
    pallas_call x1, Pallas kernels: 113 us -> 111 us  [main(): pl.pallas_call(main_kernel, out_shape=(jax.ShapeDtypeStruct((2, 512, 1024...]
    pallas_call x1, Pallas kernels: 10.5 us -> 9.07 us  [respond(): pl.pallas_call(response_kernel, out_shape=jax.ShapeDtypeStruct((8, 512, 5...]
where the time goes in v4:
time: 121 us; the launch traced here: 120 us
  Pallas kernels  120 us (99%)
    pallas_call x1, Pallas kernels, main(): pl.pallas_call(main_kernel, out_shape=(jax.ShapeDtypeStruct((2, 512, 1024...  111 us
    pallas_call x1, Pallas kernels, respond(): pl.pallas_call(response_kernel, out_shape=jax.ShapeDtypeStruct((8, 512, 5...  9.07 us

profile of v4, /device:TPU:1, one launch (start us, length us, event | category | flops | bytes accessed | tf_op | source)
XLA Modules:
  0.0 120.5 jit_solution(8684291460804336471)
XLA Ops:
  0.0 111.4 %main.1 = (bf16[2,512,1024]{2,1,0:T(8,128)(2,1)}, f32[2,1024,128]{2,1,0:T(8,128)}, bf16[4,2048,128]{2,1,0:T(8,128)(2,1)}, f32[512,128]{1,0:T(8,128)}, bf16[8,512,512]{2,1,0:T(8,128)(2,1)}) custom-call(s32[32]{0:T(128)} %occ_at.1, s32[32]{0:T(128)} %emp_at.1, bf16[8,16,4096]{2,1,0:T(8,128)(2,1)} %occ_hbm.1, bf16[16,16,4096]{2,1,0:T(8,128)(2,1)} %emp_hbm.1, ...), custom_call_target="tpu_custom_call" | custom-call | tf_op jit(solution)/shard_map/main/pallas_call | solution.py:460
  111.4 9.1 %respond.1 = bf16[8,512,512]{2,1,0:T(8,128)(2,1)} custom-call(bf16[8,512,512]{2,1,0:T(8,128)(2,1)} %get-tuple-element.10.early_ref, bf16[2,512,1024]{2,1,0:T(8,128)(2,1)} %get-tuple-element.11.turned_ref, f32[2,1024,128]{2,1,0:T(8,128)} %get-tuple-element.12.weights_ref, bf16[4,2048,128]{2,1,0:T(8,128)(2,1)} %get-tuple-element.13.proj_ref, ...), custom_call_target="tpu_custom_call" | custom-call | tf_op jit(solution)/shard_map/respond/pallas_call | solution.py:516

commit v5 on v4

--- a/solution.py
+++ b/solution.py
@@ -422,8 +422,8 @@
         next(runs[0])
     next(runs[1])
     for at in range(4):
+        next(runs[1])
         next(runs[0])
-        next(runs[1])
         if at == 1:
             turn(1)
     for _ in runs[0]:

time: 121 us -> 118 us (0.975)
  Pallas kernels: 120 us -> 118 us
    pallas_call x1, Pallas kernels: 111 us -> 109 us  [main(): pl.pallas_call(main_kernel, out_shape=(jax.ShapeDtypeStruct((2, 512, 1024...]
where the time goes in v5:
time: 118 us
  Pallas kernels  118 us (100%)
    pallas_call x1, Pallas kernels, main(): pl.pallas_call(main_kernel, out_shape=(jax.ShapeDtypeStruct((2, 512, 1024...  109 us
    pallas_call x1, Pallas kernels, respond(): pl.pallas_call(response_kernel, out_shape=jax.ShapeDtypeStruct((8, 512, 5...  9.07 us

profile of v5, /device:TPU:1, one launch (start us, length us, event | category | flops | bytes accessed | tf_op | source)
XLA Modules:
  0.0 118.1 jit_solution(1283021573997983545)
XLA Ops:
  0.0 109.0 %main.1 = (bf16[2,512,1024]{2,1,0:T(8,128)(2,1)}, f32[2,1024,128]{2,1,0:T(8,128)}, bf16[4,2048,128]{2,1,0:T(8,128)(2,1)}, f32[512,128]{1,0:T(8,128)}, bf16[8,512,512]{2,1,0:T(8,128)(2,1)}) custom-call(s32[32]{0:T(128)} %occ_at.1, s32[32]{0:T(128)} %emp_at.1, bf16[8,16,4096]{2,1,0:T(8,128)(2,1)} %occ_hbm.1, bf16[16,16,4096]{2,1,0:T(8,128)(2,1)} %emp_hbm.1, ...), custom_call_target="tpu_custom_call" | custom-call | tf_op jit(solution)/shard_map/main/pallas_call | solution.py:460
  109.0 9.1 %respond.1 = bf16[8,512,512]{2,1,0:T(8,128)(2,1)} custom-call(bf16[8,512,512]{2,1,0:T(8,128)(2,1)} %get-tuple-element.10.early_ref, bf16[2,512,1024]{2,1,0:T(8,128)(2,1)} %get-tuple-element.11.turned_ref, f32[2,1024,128]{2,1,0:T(8,128)} %get-tuple-element.12.weights_ref, bf16[4,2048,128]{2,1,0:T(8,128)(2,1)} %get-tuple-element.13.proj_ref, ...), custom_call_target="tpu_custom_call" | custom-call | tf_op jit(solution)/shard_map/respond/pallas_call | solution.py:516
